TPU v7x, 32 devices: a whole 2x2x4 slice. The times are simulated.
32 devices in a mesh: groups: 2 (over x), grid: 4 (over y, core), depth: 4 (over z).
Axes of the slice: x: 2, y: 2, z: 4, core: 2. Of those that a mesh axis runs over, the one named last changes fastest.
Arguments:
- patch_rows: bfloat16 [2048, 6144], P(('groups', 'depth'), 'grid'), parts along dimension 0, may hold values from -6 to 6
- qkv_blocks: bfloat16 [4, 3072, 3, 12, 128], P('grid'), may hold values from -0.078125 to 0.078125
- out_blocks: bfloat16 [4, 1536, 3072], P('grid'), may hold values from -0.109375 to 0.109375
- out_grad: bfloat16 [2048, 6144], P(('groups', 'depth'), 'grid'), parts along dimension 0, may hold values from -6 to 6
Outputs:
- attention_out: bfloat16 [2048, 6144], P(('groups', 'depth'), 'grid'), parts along dimension 0
- input_grad: bfloat16 [2048, 6144], P(('groups', 'depth'), 'grid'), parts along dimension 0
- qkv_grad: bfloat16 [8, 3072, 3, 12, 128], P(('groups', 'grid'), 'depth'), parts along dimension 0
- out_proj_grad: bfloat16 [8, 1536, 3072], P(('groups', 'grid'), 'depth'), parts along dimension 0
There are 2 independent parts, one for each index of `groups`. A program takes and returns all parts, laid end to end along the dimension named above; an argument that names none is the same for every part. Nothing has to cross between parts.
All inputs are finite; a program needn't handle non-finite values.
Results may differ from a plain program's by a relative error of at most 0.022.
Values may be sent and summed in bfloat16 or wider, within the bound.
No kernel may reach another device: no remote copies, remote signals or barrier semaphores. Data moves between devices by JAX's collectives and lax.ppermute only.
A program may use at most 256 MiB of HBM per device.

v0:
```python
import functools
import math

import jax
import jax.numpy as jnp
from jax import lax
from jax.experimental import pallas as pl
from jax.experimental.pallas import tpu as pltpu
from jax.sharding import PartitionSpec as P

PATCHES = 256


eps = 1e-06


def partner_2(value, axis, stride):
    mask = 2**stride
    pairs = [(source, source ^ mask) for source in range(lax.axis_size(axis))]
    return lax.ppermute(value, axis, pairs)


def normalize(vectors):
    center = vectors - jnp.mean(vectors, axis=-1, keepdims=True)
    spread = jnp.mean(center * center, axis=-1, keepdims=True)
    sigma = jnp.sqrt(spread + eps)
    return (center / sigma, sigma)


def normalize_back(grads, normed, sigma):
    first_mean = jnp.mean(grads, axis=-1, keepdims=True)
    second_mean = jnp.mean(grads * normed, axis=-1, keepdims=True)
    return (grads - first_mean - normed * second_mean) / sigma


def collect_panel(pieces, first_bit, count, position, along):
    for section in range(count):
        partner = partner_2(pieces, "grid", first_bit + section)
        higher = position >> section & 1
        pieces = jnp.where(
            higher == 1,
            jnp.concatenate([partner, pieces], along),
            jnp.concatenate([pieces, partner], along),
        )
    return pieces


def reduce_panel(partial_sum, first_bit, count, position, along):
    for section in reversed(range(count)):
        half_size = partial_sum.shape[along] // 2
        higher = position >> section & 1
        kept = lax.dynamic_slice_in_dim(partial_sum, higher * half_size, half_size, along)
        outgoing = lax.dynamic_slice_in_dim(partial_sum, (1 - higher) * half_size, half_size, along)
        partial_sum = kept + partner_2(
            outgoing.astype(jnp.bfloat16), "grid", first_bit + section
        ).astype(outgoing.dtype)
    return partial_sum


def contract(left, right, left_dim, right_dim):
    return lax.dot_general(
        left, right, (((left_dim,), (right_dim,)), ((), ())), preferred_element_type=jnp.float32
    )


def local(patch_rows, qkv_blocks, out_blocks, out_grad):
    side = math.isqrt(lax.axis_size("grid"))
    bit_count = side.bit_length() - 1
    grid_index = lax.axis_index("grid")
    row_place = grid_index // side
    col_place = grid_index % side
    slice_rows = patch_rows.shape[0]
    block_width = qkv_blocks.shape[1]
    heads_local = qkv_blocks.shape[3]
    head_dim = qkv_blocks.shape[4]
    width_local = heads_local * head_dim
    query_rows = slice_rows // side
    scale = head_dim ** (-0.5)
    x_panel = collect_panel(patch_rows, 0, bit_count, col_place, 1)
    w_in = qkv_blocks[0].reshape(block_width, 3 * width_local)
    partial_proj = jnp.dot(x_panel, w_in, preferred_element_type=jnp.float32)
    proj_local = reduce_panel(partial_proj, bit_count, bit_count, row_place, 0)
    proj_local = proj_local.reshape(query_rows, 3, heads_local, head_dim)
    query_raw = proj_local[:, 0]
    k_hat, k_sigma = normalize(proj_local[:, 1])
    kv_local = jnp.stack(
        [k_hat.astype(jnp.bfloat16), proj_local[:, 2].astype(jnp.bfloat16)], axis=1
    )
    kv_gathered = collect_panel(kv_local, bit_count, bit_count, row_place, 0)
    keys_all = kv_gathered[:, 0]
    values_all = kv_gathered[:, 1]
    q_hat, q_sigma = normalize(query_raw)
    queries = q_hat.astype(jnp.bfloat16)
    group_count = max(1, query_rows // PATCHES)
    key_rows = max(query_rows, PATCHES)
    group_shape = (group_count, key_rows // group_count, heads_local, head_dim)
    keys = keys_all.reshape(group_shape)
    values = values_all.reshape(group_shape)
    query_group = queries.reshape(group_count, query_rows // group_count, heads_local, head_dim)
    scores = (
        jnp.einsum("gqhe,gkhe->ghqk", query_group, keys, preferred_element_type=jnp.float32) * scale
    )
    expo = jnp.exp(scores)
    probs = expo / jnp.sum(expo, axis=-1, keepdims=True)
    probs_low = probs.astype(jnp.bfloat16)
    attended = jnp.einsum("ghqk,gkhe->gqhe", probs_low, values, preferred_element_type=jnp.float32)
    attended = attended.astype(jnp.bfloat16).reshape(query_rows, width_local)
    attended_panel = collect_panel(attended, bit_count, bit_count, row_place, 0)
    w_back = out_blocks[0]
    out_partial = jnp.dot(attended_panel, w_back, preferred_element_type=jnp.float32)
    attention_out = reduce_panel(out_partial, 0, bit_count, col_place, 1).astype(jnp.bfloat16)
    grad_panel = collect_panel(out_grad, 0, bit_count, col_place, 1)
    d_att_partial = contract(grad_panel, w_back, 1, 1)
    d_attended = reduce_panel(d_att_partial, bit_count, bit_count, row_place, 0).astype(
        jnp.bfloat16
    )
    d_attended = d_attended.reshape(group_count, query_rows // group_count, heads_local, head_dim)
    grad_out_part = contract(attended_panel, grad_panel, 0, 0)
    d_probs = jnp.einsum("gqhe,gkhe->ghqk", d_attended, values, preferred_element_type=jnp.float32)
    d_values = jnp.einsum(
        "ghqk,gqhe->gkhe", probs_low, d_attended, preferred_element_type=jnp.float32
    )
    d_scores = (probs * (d_probs - jnp.sum(probs * d_probs, axis=-1, keepdims=True))).astype(
        jnp.bfloat16
    )
    d_queries = (
        jnp.einsum("ghqk,gkhe->gqhe", d_scores, keys, preferred_element_type=jnp.float32) * scale
    )
    d_keys = (
        jnp.einsum("ghqk,gqhe->gkhe", d_scores, query_group, preferred_element_type=jnp.float32)
        * scale
    )
    key_terms = jnp.stack(
        [
            d_keys.reshape(key_rows, heads_local, head_dim),
            d_values.reshape(key_rows, heads_local, head_dim),
        ],
        axis=1,
    )
    key_sums = reduce_panel(key_terms, bit_count, bit_count, row_place, 0)
    dq_raw = normalize_back(d_queries.reshape(query_rows, heads_local, head_dim), q_hat, q_sigma)
    dk_raw = normalize_back(key_sums[:, 0], k_hat, k_sigma)
    d_proj = (
        jnp.stack([dq_raw, dk_raw, key_sums[:, 1]], axis=1)
        .astype(jnp.bfloat16)
        .reshape(query_rows, 3 * width_local)
    )
    d_proj_panel = collect_panel(d_proj, bit_count, bit_count, row_place, 0)
    input_partial = contract(d_proj_panel, w_in, 1, 1)
    input_grad = reduce_panel(input_partial, 0, bit_count, col_place, 1).astype(jnp.bfloat16)
    grad_in_part = contract(x_panel, d_proj_panel, 0, 0)
    grad_in, grad_out = (
        lax.psum_scatter(
            grad_in_part.astype(jnp.bfloat16), "depth", scatter_dimension=0, tiled=True
        ).astype(jnp.float32),
        lax.psum_scatter(
            grad_out_part.astype(jnp.bfloat16), "depth", scatter_dimension=0, tiled=True
        ).astype(jnp.float32),
    )
    qkv_grad = grad_in.astype(jnp.bfloat16).reshape(1, grad_in.shape[0], 3, heads_local, head_dim)
    out_proj_grad = grad_out.astype(jnp.bfloat16)[None]
    return (attention_out, input_grad, qkv_grad, out_proj_grad)


SIZES = [6]
HINT = 4096


def y_swap(value):
    return partner_2(value, "grid", 1)


def core_swap(value):
    return partner_2(value, "grid", 0)


def hint(flops, bytes_accessed, transcendentals):
    return pl.CostEstimate(
        flops=flops // HINT, bytes_accessed=bytes_accessed // HINT, transcendentals=transcendentals
    )


def params(*semantics):
    return pltpu.CompilerParams(dimension_semantics=semantics, vmem_limit_bytes=56 * 2**20)


def proj_kernel(place_ref, own_ref, other_ref, w_own_ref, w_other_ref, out_ref):
    heads = w_own_ref.shape[1]
    columns = [(part, head) for head in range(heads) for part in range(3)]
    w_own = jnp.concatenate([w_own_ref[part, head] for part, head in columns], axis=1)
    total = jnp.dot(own_ref[...], w_own, preferred_element_type=jnp.float32)
    w_other = jnp.concatenate([w_other_ref[part, head] for part, head in columns], axis=1)
    total += jnp.dot(other_ref[...], w_other, preferred_element_type=jnp.float32)
    out_ref[...] = total.astype(out_ref.dtype)


def project(place, x_own, x_other, weights, swap, start, heads, kind):
    rows, piece = x_own.shape
    head_dim = weights.shape[3]
    group = 2 if heads % 2 == 0 and start % 2 == 0 else 1
    if start % 3 == 0 and heads % 3 == 0:
        group = 3
    per_half = weights.shape[1] // 2 // group
    width = heads * 3 * head_dim

    def head_block(step, place):
        return (place[0] + swap) % 2 * per_half + start // group + step

    whole = pl.BlockSpec((rows, piece), lambda step, place: (0, 0))
    block = (3, group, piece, head_dim)
    return pl.pallas_call(
        proj_kernel,
        grid_spec=pltpu.PrefetchScalarGridSpec(
            num_scalar_prefetch=1,
            grid=(heads // group,),
            in_specs=[
                whole,
                whole,
                pl.BlockSpec(block, lambda step, place: (0, head_block(step, place), place[1], 0)),
                pl.BlockSpec(
                    block, lambda step, place: (0, head_block(step, place), 1 - place[1], 0)
                ),
            ],
            out_specs=pl.BlockSpec((rows, group * 3 * head_dim), lambda step, place: (0, step)),
        ),
        out_shape=jax.ShapeDtypeStruct((rows, width), kind),
        compiler_params=params("arbitrary"),
        cost_estimate=hint(
            flops=4 * rows * piece * width,
            bytes_accessed=4 * piece * width + 4 * rows * piece + 4 * rows * width,
            transcendentals=0,
        ),
        name="project",
    )(place, x_own, x_other, weights, weights)


def attention_kernel(scale, keep_ref, recv_ref, d_out_ref, att_ref, d_proj_ref):
    head_dim = d_out_ref.shape[1]
    low = jnp.bfloat16

    def part(index):
        columns = slice(index * head_dim, (index + 1) * head_dim)
        return keep_ref[:, columns] + recv_ref[:, columns].astype(jnp.float32)

    def dot(left, right, left_dim, right_dim):
        return contract(left, right, left_dim, right_dim)

    q_hat, q_sigma = normalize(part(0))
    k_hat, k_sigma = normalize(part(1))
    queries, keys, values = q_hat.astype(low), k_hat.astype(low), part(2).astype(low)
    d_out = d_out_ref[...]
    expo = jnp.exp(dot(queries, keys, 1, 1) * scale)
    probs = expo / jnp.sum(expo, axis=-1, keepdims=True)
    probs_low = probs.astype(low)
    att_ref[...] = dot(probs_low, values, 1, 0).astype(low)
    d_probs = dot(d_out, values, 1, 1)
    d_values = dot(probs_low, d_out, 0, 0)
    weighted = probs * d_probs
    d_scores = (weighted - probs * jnp.sum(weighted, axis=-1, keepdims=True)).astype(low)
    d_queries = dot(d_scores, keys, 1, 0) * scale
    d_keys = dot(d_scores, queries, 0, 0) * scale
    d_proj_ref[:, :head_dim] = normalize_back(d_queries, q_hat, q_sigma).astype(low)
    d_proj_ref[:, head_dim : 2 * head_dim] = normalize_back(d_keys, k_hat, k_sigma).astype(low)
    d_proj_ref[:, 2 * head_dim :] = d_values.astype(low)


def attend(keep, recv, d_attended, start, heads, head_dim):
    rows = keep.shape[0]
    triple = pl.BlockSpec((rows, 3 * head_dim), lambda head: (0, head))
    single = pl.BlockSpec((rows, head_dim), lambda head: (0, head))
    return pl.pallas_call(
        functools.partial(attention_kernel, head_dim ** (-0.5)),
        grid=(heads,),
        in_specs=[triple, triple, pl.BlockSpec((rows, head_dim), lambda head: (0, start + head))],
        out_specs=[single, triple],
        out_shape=[
            jax.ShapeDtypeStruct((rows, heads * head_dim), jnp.bfloat16),
            jax.ShapeDtypeStruct((rows, heads * 3 * head_dim), jnp.bfloat16),
        ],
        compiler_params=params("arbitrary"),
        cost_estimate=hint(
            flops=14 * heads * rows * rows * head_dim,
            bytes_accessed=28 * heads * rows * head_dim,
            transcendentals=0,
        ),
        name="attend",
    )(keep, recv, d_attended)


def input_kernel(place_ref, d_own_ref, d_other_ref, w_own_ref, w_other_ref, *refs):
    keep_ref, send_ref, acc_own_ref, acc_other_ref = refs
    step, steps = pl.program_id(0), pl.num_programs(0)
    heads = w_own_ref.shape[1]
    columns = [(part, head) for head in range(heads) for part in range(3)]

    @pl.when(step == 0)
    def _():
        acc_own_ref[...] = jnp.zeros_like(acc_own_ref)
        acc_other_ref[...] = jnp.zeros_like(acc_other_ref)

    def add(grads):
        for w_ref, acc_ref in ((w_own_ref, acc_own_ref), (w_other_ref, acc_other_ref)):
            w = jnp.concatenate([w_ref[part, head] for part, head in columns], axis=1)
            acc_ref[...] += contract(w, grads, 1, 1)

    @pl.when(step < steps // 2)
    def _():
        add(d_own_ref[...])

    @pl.when(step >= steps // 2)
    def _():
        add(d_other_ref[...])

    @pl.when(step == steps - 1)
    def _():
        keep_ref[...] = acc_own_ref[...].T
        send_ref[...] = acc_other_ref[...].T.astype(send_ref.dtype)


def input_terms(place, d_own, d_other, weights):
    rows, width = d_own.shape
    head_dim = weights.shape[3]
    piece = weights.shape[2] // 2
    heads_half = weights.shape[1] // 2
    group = 2 if heads_half % 2 == 0 else 1
    steps = heads_half // group

    def head_block(step, place):
        return (place[0] + step // steps) % 2 * steps + step % steps

    block = (3, group, piece, head_dim)
    total = pl.BlockSpec((rows, piece), lambda step, place: (0, 0))
    grads = (rows, group * 3 * head_dim)
    return pl.pallas_call(
        input_kernel,
        grid_spec=pltpu.PrefetchScalarGridSpec(
            num_scalar_prefetch=1,
            grid=(2 * steps,),
            in_specs=[
                pl.BlockSpec(grads, lambda step, place: (0, jnp.minimum(step, steps - 1))),
                pl.BlockSpec(grads, lambda step, place: (0, jnp.maximum(step - steps, 0))),
                pl.BlockSpec(block, lambda step, place: (0, head_block(step, place), place[1], 0)),
                pl.BlockSpec(
                    block, lambda step, place: (0, head_block(step, place), 1 - place[1], 0)
                ),
            ],
            out_specs=[total, total],
            scratch_shapes=[pltpu.VMEM((piece, rows), jnp.float32)] * 2,
        ),
        out_shape=[
            jax.ShapeDtypeStruct((rows, piece), jnp.float32),
            jax.ShapeDtypeStruct((rows, piece), jnp.bfloat16),
        ],
        compiler_params=params("arbitrary"),
        cost_estimate=hint(
            flops=8 * rows * piece * width,
            bytes_accessed=8 * piece * width + 10 * rows * piece,
            transcendentals=0,
        ),
        name="input_terms",
    )(place, d_own, d_other, weights, weights)


def weight_kernel(count, place_ref, x_ref, *refs):
    slots, out_ref, x_sorted = refs[:count], refs[-2], refs[-1]
    heads, head_dim = out_ref.shape[1], out_ref.shape[3]
    patches = x_ref.shape[0] // count

    @pl.when(pl.program_id(0) == 0)
    def _():
        for slot in range(count):
            offset = pl.multiple_of(place_ref[2 + slot] * patches, patches)
            x_sorted[:, slot * patches : (slot + 1) * patches] = x_ref[pl.ds(offset, patches), :].T

    grads = jnp.concatenate([slot_ref[...] for slot_ref in slots], axis=0)
    total = jnp.dot(x_sorted[...], grads, preferred_element_type=jnp.float32)
    for head in range(heads):
        for part in range(3):
            column = (head * 3 + part) * head_dim
            out_ref[part, head] = total[:, column : column + head_dim].astype(out_ref.dtype)


def weight_terms(place, x_slots, slots, swap, start, shape, filled):
    count = len(slots)
    rows, width = slots[0].shape
    block_rows = x_slots.shape[1]
    head_dim = shape[3]
    heads = width // (3 * head_dim)
    group = 2 if heads % 2 == 0 and start % 2 == 0 else 1
    per_half = shape[1] // 2 // group
    part = pl.BlockSpec((rows, group * 3 * head_dim), lambda step, place: (0, step))
    filled = () if filled is None else (filled,)
    return pl.pallas_call(
        functools.partial(weight_kernel, count),
        grid_spec=pltpu.PrefetchScalarGridSpec(
            num_scalar_prefetch=1,
            grid=(heads // group,),
            in_specs=[pl.BlockSpec(x_slots.shape, lambda step, place: (0, 0))]
            + [part] * count
            + [pl.BlockSpec(memory_space=pl.ANY)] * len(filled),
            out_specs=pl.BlockSpec(
                (3, group, block_rows, head_dim),
                lambda step, place: (
                    0,
                    (place[0] + swap) % 2 * per_half + start // group + step,
                    0,
                    0,
                ),
            ),
            scratch_shapes=[pltpu.VMEM(x_slots.shape[::-1], x_slots.dtype)],
        ),
        out_shape=jax.ShapeDtypeStruct(shape, jnp.bfloat16),
        input_output_aliases={2 + count: 0} if filled else {},
        compiler_params=params("arbitrary"),
        cost_estimate=hint(
            flops=2 * count * rows * block_rows * width,
            bytes_accessed=2 * count * rows * (block_rows + width) + 2 * block_rows * width,
            transcendentals=0,
        ),
        name="weight_terms",
    )(place, x_slots, *slots, *filled)


def out_kernel(count, place_ref, att_ref, *refs):
    own, other, out_ref, att_turned = refs[:count], refs[count : 2 * count], refs[-2], refs[-1]

    @pl.when(pl.program_id(0) == 0)
    def _():
        att_turned[...] = att_ref[...].T

    def fill(slots):
        grads = jnp.concatenate([slot_ref[...] for slot_ref in slots], axis=0)
        total = jnp.dot(att_turned[...], grads, preferred_element_type=jnp.float32)
        out_ref[...] = total.astype(out_ref.dtype)

    half = pl.num_programs(0) // 2

    @pl.when(pl.program_id(0) < half)
    def _():
        fill(own)

    @pl.when(pl.program_id(0) >= half)
    def _():
        fill(other)


def out_terms(place, att_slots, own, other):
    count = len(own)
    width = own[0].shape[1]
    steps = 2 if width % 256 == 0 else 1
    block = width // steps
    rows, block_rows = att_slots.shape
    return pl.pallas_call(
        functools.partial(out_kernel, count),
        grid_spec=pltpu.PrefetchScalarGridSpec(
            num_scalar_prefetch=1,
            grid=(2 * steps,),
            in_specs=[pl.BlockSpec((rows, block_rows), lambda step, place: (0, 0))]
            + [
                pl.BlockSpec(
                    (slot.shape[0], block),
                    lambda step, place: (0, jnp.minimum(step, steps - 1)),
                )
                for slot in own
            ]
            + [
                pl.BlockSpec(
                    (slot.shape[0], block),
                    lambda step, place: (0, jnp.maximum(step - steps, 0)),
                )
                for slot in other
            ],
            out_specs=pl.BlockSpec(
                (block_rows, block),
                lambda step, place: (
                    0,
                    (place[1] + step // steps) % 2 * steps + step % steps,
                ),
            ),
            scratch_shapes=[pltpu.VMEM((block_rows, rows), att_slots.dtype)],
        ),
        out_shape=jax.ShapeDtypeStruct((block_rows, 2 * width), jnp.bfloat16),
        compiler_params=params("arbitrary"),
        cost_estimate=hint(
            flops=4 * rows * block_rows * width,
            bytes_accessed=4 * rows * width + 2 * block_rows * (rows + 2 * width),
            transcendentals=0,
        ),
        name="out_terms",
    )(place, att_slots, *own, *other)


def output_kernel(place_ref, own_ref, other_ref, v_own_ref, v_other_ref, keep_ref, send_ref):
    total = jnp.dot(own_ref[...], v_own_ref[...], preferred_element_type=jnp.float32)
    total += jnp.dot(other_ref[...], v_other_ref[...], preferred_element_type=jnp.float32)

    @pl.when(pl.program_id(0) == 0)
    def _():
        send_ref[...] = total.astype(send_ref.dtype)

    @pl.when(pl.program_id(0) == 1)
    def _():
        keep_ref[...] = total


def output_terms(place, att_own, att_other, w_back):
    rows, half = att_own.shape
    piece = w_back.shape[1] // 2
    whole = pl.BlockSpec((rows, half), lambda step, place: (0, 0))
    result = pl.BlockSpec((rows, piece), lambda step, place: (0, 0))
    return pl.pallas_call(
        output_kernel,
        grid_spec=pltpu.PrefetchScalarGridSpec(
            num_scalar_prefetch=1,
            grid=(2,),
            in_specs=[
                whole,
                whole,
                pl.BlockSpec(
                    (half, piece), lambda step, place: (place[0], (place[1] + 1 + step) % 2)
                ),
                pl.BlockSpec(
                    (half, piece), lambda step, place: (1 - place[0], (place[1] + 1 + step) % 2)
                ),
            ],
            out_specs=[result, result],
        ),
        out_shape=[
            jax.ShapeDtypeStruct((rows, piece), jnp.float32),
            jax.ShapeDtypeStruct((rows, piece), jnp.bfloat16),
        ],
        compiler_params=params("arbitrary"),
        cost_estimate=hint(
            flops=8 * rows * half * piece,
            bytes_accessed=8 * half * piece + 4 * rows * half + 6 * rows * piece,
            transcendentals=0,
        ),
        name="output_terms",
    )(place, att_own, att_other, w_back, w_back)


def ordered(place, own, other, along):
    return jnp.where(
        place == 0,
        jnp.concatenate([own, other], along),
        jnp.concatenate([other, own], along),
    )


def line_step(upper, lower, axis):
    count = lax.axis_size(axis)
    step = len(upper)
    upper.append(lax.ppermute(upper[-1], axis, [(d + 1, d) for d in range(count - step)]))
    lower.append(lax.ppermute(lower[-1], axis, [(d - 1, d) for d in range(step, count)]))


def together(*groups):
    flat, tree = jax.tree.flatten(groups)
    return jax.tree.unflatten(tree, lax.optimization_barrier(flat))


def by_offset(upper, lower, axis):
    count = lax.axis_size(axis)
    place = lax.axis_index(axis)
    return [
        jnp.where(place + slot < count, upper[slot], lower[count - slot])
        for slot in range(1, count)
    ]


def arrivals(count):
    table = []
    for place in range(count):
        found = []
        for step in range(1, count):
            found += [(0, step)] * (place + step < count) + [(1, step)] * (place >= step)
        if place >= count // 2:
            found.sort(key=lambda item: (item[1], -item[0]))
        table.append(found)
    return table


def pick_arrival(upper, lower, index, table, axis):
    place = lax.axis_index(axis)
    picked = None
    for other, found in enumerate(table):
        side, step = found[index]
        source = (upper, lower)[side][step]
        picked = source if picked is None else jnp.where(place == other, source, picked)
    return picked


def send_slots(blocks_of, axis):
    count = lax.axis_size(axis)
    place = lax.axis_index(axis)
    slots = [blocks_of(place)]
    for slot in range(1, count):
        target = (place + count - slot) % count
        pairs = [(d, (d + count - slot) % count) for d in range(count)]
        slots.append(lax.ppermute(blocks_of(target), axis, pairs))
    return slots


def local_heads(patch_rows, qkv_blocks, out_blocks, out_grad):
    depth = lax.axis_size("depth")
    grid_index = lax.axis_index("grid")
    row_place, col_place = grid_index // 2, grid_index % 2
    depth_place = lax.axis_index("depth")
    table = arrivals(depth)
    offsets = [0] + [
        sum(
            jnp.where(depth_place == d, (step if side == 0 else depth - step), 0)
            for d, (side, step) in enumerate(table[d][index] for d in range(depth))
        )
        for index in range(depth - 1)
    ]
    place = jnp.stack([row_place, col_place, *offsets]).astype(jnp.int32)
    heads_local, head_dim = qkv_blocks.shape[3:]
    heads_half = heads_local // 2
    half = heads_half * head_dim
    weights = qkv_blocks[0].transpose(1, 2, 0, 3)
    w_back = out_blocks[0]
    low = jnp.bfloat16
    sizes = SIZES if heads_half == sum(SIZES) else [heads_half]
    chunks = [(sum(sizes[:index]), size) for index, size in enumerate(sizes)]

    x_other = core_swap(patch_rows)
    g_other = core_swap(out_grad)
    received = []
    for start, heads in chunks:
        send = project(place, patch_rows, x_other, weights, 1, start, heads, low)
        received.append(y_swap(send))
    g_line = ([out_grad], [out_grad])
    line_step(*g_line, "depth")
    line_step(*g_line, "depth")
    grad_panel = ordered(col_place, out_grad, g_other, 1)
    d_att_partial = contract(grad_panel, w_back, 1, 1)
    d_att_send = lax.dynamic_slice_in_dim(d_att_partial, (1 - row_place) * half, half, 1)
    d_att_keep = lax.dynamic_slice_in_dim(d_att_partial, row_place * half, half, 1)
    d_attended = (d_att_keep + y_swap(d_att_send.astype(low)).astype(jnp.float32)).astype(low)

    x_panel = ordered(col_place, patch_rows, x_other, 1)
    block_rows = x_panel.shape[1] // depth
    part_rows = block_rows // 2
    x_parts = send_slots(
        lambda target: lax.dynamic_slice_in_dim(
            x_panel, target * block_rows + col_place * part_rows, part_rows, 1
        ),
        "depth",
    )

    shape = (3, heads_local, block_rows, head_dim)
    attended, d_proj = [], []
    for (start, heads), recv in zip(chunks, received):
        keep = project(place, patch_rows, x_other, weights, 0, start, heads, jnp.float32)
        parts = attend(keep, recv, d_attended, start, heads, head_dim)
        attended.append(parts[0])
        d_proj.append(parts[1])
    attended, d_proj = jnp.concatenate(attended, axis=1), jnp.concatenate(d_proj, axis=1)

    d_proj, g_line = together(d_proj, g_line)
    upper, lower = [d_proj], [d_proj]
    own, other = [d_proj], [y_swap(d_proj)]
    attended_other = y_swap(attended)

    line_step(upper, lower, "depth")
    slot = pick_arrival(upper, lower, 0, table, "depth")
    x_part = jnp.concatenate(x_parts, axis=0)
    x_slots = ordered(col_place, x_part, core_swap(x_part), 1)
    upper, lower, slot, other, x_slots, attended_other = together(
        upper, lower, slot, other, x_slots, attended_other
    )
    own.append(slot)
    other.append(y_swap(slot))

    line_step(upper, lower, "depth")
    slot = pick_arrival(upper, lower, 1, table, "depth")
    input_keep, input_send = input_terms(place, own[0], other[0], weights)
    upper, lower, slot, other, input_keep, input_send = together(
        upper, lower, slot, other, input_keep, input_send
    )
    own.append(slot)
    other.append(y_swap(slot))

    line_step(upper, lower, "depth")
    input_grad = (input_keep + core_swap(input_send).astype(jnp.float32)).astype(low)
    slot = pick_arrival(upper, lower, 2, table, "depth")
    attended_panel = ordered(row_place, attended, attended_other, 1)
    out_keep, out_send = output_terms(place, attended, attended_other, w_back)
    slot, x_slots, input_grad, attended_panel, g_line, out_keep, out_send = together(
        slot, x_slots, input_grad, attended_panel, g_line, out_keep, out_send
    )
    own.append(slot)
    other.append(y_swap(slot))

    line_step(*g_line, "depth")
    grad_rows = w_back.shape[0] // depth
    a_slots = send_slots(
        lambda target: lax.dynamic_slice_in_dim(
            attended_panel, target * grad_rows, grad_rows, 1
        ),
        "depth",
    )
    attention_out = (out_keep + core_swap(out_send).astype(jnp.float32)).astype(low)
    filled = weight_terms(place, x_slots, own, 0, 0, shape, None)
    other, g_line, a_slots, attention_out, filled = together(
        other, g_line, a_slots, attention_out, filled
    )

    g_far = jnp.concatenate(by_offset(*g_line, "depth"), axis=0)
    g_far_other = core_swap(g_far)
    filled = weight_terms(place, x_slots, other, 1, 0, shape, filled)
    out_proj_grad = out_terms(
        place,
        jnp.concatenate(a_slots, axis=0),
        [out_grad, g_far],
        [g_other, g_far_other],
    )
    qkv_grad = filled.transpose(2, 0, 1, 3)[None]
    return (attention_out, input_grad, qkv_grad, out_proj_grad[None])


def local_any(patch_rows, qkv_blocks, out_blocks, out_grad):
    by_heads = (
        lax.axis_size("grid") == 4
        and qkv_blocks.shape[3] % 2 == 0
        and patch_rows.shape[0] == PATCHES
        and qkv_blocks.shape[1] % (2 * lax.axis_size("depth")) == 0
        and out_blocks.shape[1] % lax.axis_size("depth") == 0
        and lax.axis_size("depth") == 4
    )
    body = local_heads if by_heads else local
    return body(patch_rows, qkv_blocks, out_blocks, out_grad)


def solution(mesh):
    return jax.shard_map(
        local_any,
        mesh=mesh,
        in_specs=(
            P(("groups", "depth"), "grid"),
            P("grid", None, None, None, None),
            P("grid", None, None),
            P(("groups", "depth"), "grid"),
        ),
        out_specs=(
            P(("groups", "depth"), "grid"),
            P(("groups", "depth"), "grid"),
            P(("groups", "grid"), "depth", None, None, None),
            P(("groups", "grid"), "depth", None),
        ),
        check_vma=False,
    )
```

profile of v0, /device:TPU:0, one launch (start us, length us, event | category | flops | bytes accessed | tf_op | source)
XLA Modules:
  0.0 241.7 jit_solution(6307454404385917782)
XLA Ops:
  2.4 5.2 %collective-permute-start.6 = (bf16[256,1536]{1,0:T(8,128)(2,1)}, bf16[256,1536]{1,0:T(8,128)(2,1)S(1)}, u32[]{:S(2)}, u32[]{:S(2)}) collective-permute-start(bf16[256,1536]{1,0:T(8,128)(2,1)} %refs_0_.1), channel_id=1, source_target_pairs={{0,1},{1,2},{2,3},{4,5},{5,6},{6,7},{8,9},{9,10},{10,11},{12,13},{... | collective-permute-start | bytes 2359304 | tf_op jit(solution)/shard_map/ppermute | solution.py:554
  9.4 9.5 %project.3 = bf16[256,2304]{1,0:T(8,128)(2,1)} custom-call(s32[6]{0:T(128)} %stack.23.place_ref, bf16[256,1536]{1,0:T(8,128)(2,1)} %own_ref.3, bf16[256,1536]{1,0:T(8,128)(2,1)} %copy-done.2, bf16[3,12,3072,128]{3,2,1,0:T(8,128)(2,1)} %bitcast.15, bf16[3,12,3072,128]{3,2,1,0:T(8,128)(2,1)} %bitcast.16), custom_call_target="tpu_custom_call" | custom-call | flops 884736 | bytes 4416 | tf_op jit(solution)/shard_map/project/pallas_call | solution.py:211
  20.9 3.1 %collective-permute-done.4 = bf16[256,1536]{1,0:T(8,128)(2,1)S(1)} collective-permute-done((bf16[256,1536]{1,0:T(8,128)(2,1)}, bf16[256,1536]{1,0:T(8,128)(2,1)S(1)}, u32[]{:S(2)}, u32[]{:S(2)}) %collective-permute-start.4) | collective-permute-done | bytes 786464 | tf_op jit(solution)/shard_map/ppermute | solution.py:553
  26.1 6.6 %fusion = f32[256,1536]{1,0:T(8,128)S(1)} fusion(bf16[256,1536]{1,0:T(8,128)(2,1)S(1)} %collective-permute-done.2.refs_2_, bf16[256,1536]{1,0:T(8,128)(2,1)S(1)} %copy-done.17, pred[]{:T(512)S(6)} %eq.24, bf16[1,1536,3072]{2,1,0:T(8,128)(2,1)} %param.6), kind=kOutput, calls=%fused_computation.3 | convolution fusion | flops 2422996992 | bytes 12582913 | tf_op jit(solution)/shard_map/dot_general | solution.py:61
  35.0 5.0 %collective-permute-start.11 = (bf16[256,384]{1,0:T(8,128)(2,1)S(1)}, bf16[256,384]{1,0:T(8,128)(2,1)S(1)}, u32[]{:S(2)}, u32[]{:S(2)}) collective-permute-start(bf16[256,384]{1,0:T(8,128)(2,1)S(1)} %get-tuple-element.107), channel_id=1, source_target_pairs={{0,3},{1,0},{2,1},{3,2},{4,7},{5,4},{6,5},{7,6},{8,11},{9,8},{10,9... | collective-permute-start | bytes 589832 | tf_op jit(solution)/shard_map/ppermute | solution.py:600
  40.1 9.6 %project.2.keep_ref = f32[256,2304]{1,0:T(8,128)} custom-call(s32[6]{0:T(128)} %stack.23.place_ref, bf16[256,1536]{1,0:T(8,128)(2,1)} %own_ref.3, bf16[256,1536]{1,0:T(8,128)(2,1)} %copy-done.2, bf16[3,12,3072,128]{3,2,1,0:T(8,128)(2,1)} %bitcast.17, bf16[3,12,3072,128]{3,2,1,0:T(8,128)(2,1)} %bitcast.18), custom_call_target="tpu_custom_call" | custom-call | flops 884736 | bytes 4416 | tf_op jit(solution)/shard_map/project/pallas_call | solution.py:211
  49.7 6.4 %collective-permute-done.3 = bf16[256,768]{1,0:T(8,128)(2,1)S(1)} collective-permute-done((bf16[256,768]{1,0:T(8,128)(2,1)S(1)}, bf16[256,768]{1,0:T(8,128)(2,1)S(1)}, u32[]{:S(2)}, u32[]{:S(2)}) %collective-permute-start.3) | collective-permute-done | bytes 393248 | tf_op jit(solution)/shard_map/ppermute | solution.py:20
  56.1 2.8 %collective-permute-start.12 = (bf16[256,384]{1,0:T(8,128)(2,1)S(1)}, bf16[256,384]{1,0:T(8,128)(2,1)S(1)}, u32[]{:S(2)}, u32[]{:S(2)}) collective-permute-start(bf16[256,384]{1,0:T(8,128)(2,1)S(1)} %get-tuple-element.106), channel_id=1, source_target_pairs={{0,2},{1,3},{2,0},{3,1},{4,6},{5,7},{6,4},{7,5},{8,10},{9,11},{10,... | collective-permute-start | bytes 589832 | tf_op jit(solution)/shard_map/ppermute | solution.py:600
  60.0 8.7 %attend.1 = (bf16[256,768]{1,0:T(8,128)(2,1)}, bf16[256,2304]{1,0:T(8,128)(2,1)}) custom-call(f32[256,2304]{1,0:T(8,128)} %project.2.keep_ref, bf16[256,2304]{1,0:T(8,128)(2,1)} %copy-done.16, bf16[256,768]{1,0:T(8,128)(2,1)} %add_convert_fusion.2.d_out_ref), custom_call_target="tpu_custom_call" | custom-call | flops 172032 | bytes 1344 | tf_op jit(solution)/shard_map/attend/pallas_call | solution.py:271
  70.2 4.8 %collective-permute-start.9 = (bf16[256,2304]{1,0:T(8,128)(2,1)}, bf16[256,2304]{1,0:T(8,128)(2,1)S(1)}, u32[]{:S(2)}, u32[]{:S(2)}) collective-permute-start(bf16[256,2304]{1,0:T(8,128)(2,1)} %get-tuple-element.55.d_own_ref.refs_0_), channel_id=1, source_target_pairs={{0,1},{1,2},{2,3},{4,5},{5,6},{6,7},{8,9},{9,10},{10,11},{12,13},{... | collective-permute-start | bytes 3538952 | tf_op jit(solution)/shard_map/ppermute | solution.py:554
  77.5 10.0 %maximum_select_fusion.3.x_ref = bf16[1024,768]{1,0:T(8,128)(2,1)} fusion(bf16[1024,384]{1,0:T(8,128)(2,1)S(1)} %collective-permute-done.14, bf16[256,384]{1,0:T(8,128)(2,1)S(1)} %collective-permute-done.13, bf16[256,384]{1,0:T(8,128)(2,1)S(1)} %collective-permute-done.12, bf16[256,384]{1,0:T(8,128)(2,1)S(1)} %collective-permute-done.11, ...), kind=kLoop, calls=%fused_computation.10 | loop fusion | flops 16515072 | bytes 3145729 | tf_op jit(solution)/shard_map/jit(_where)/select_n | solution.py:543
  89.0 9.2 %collective-permute-done.8 = bf16[256,2304]{1,0:T(8,128)(2,1)S(1)} collective-permute-done((bf16[256,2304]{1,0:T(8,128)(2,1)}, bf16[256,2304]{1,0:T(8,128)(2,1)S(1)}, u32[]{:S(2)}, u32[]{:S(2)}) %collective-permute-start.8) | collective-permute-done | bytes 1179680 | tf_op jit(solution)/shard_map/ppermute | solution.py:553
  99.6 12.5 %collective-permute-done.15.other_ref = bf16[256,768]{1,0:T(8,128)(2,1)S(1)} collective-permute-done((bf16[256,768]{1,0:T(8,128)(2,1)S(1)}, bf16[256,768]{1,0:T(8,128)(2,1)S(1)}, u32[]{:S(2)}, u32[]{:S(2)}) %collective-permute-start.15) | collective-permute-done | bytes 393248 | tf_op jit(solution)/shard_map/ppermute | solution.py:20
  115.7 16.8 %input_terms.1 = (f32[256,1536]{1,0:T(8,128)}, bf16[256,1536]{1,0:T(8,128)(2,1)}) custom-call(s32[6]{0:T(128)} %stack.23.place_ref, bf16[256,2304]{1,0:T(8,128)(2,1)} %get-tuple-element.55.d_own_ref.refs_0_, bf16[256,2304]{1,0:T(8,128)(2,1)} %copy-done.6, bf16[3,12,3072,128]{3,2,1,0:T(8,128)(2,1)} %bitcast.19, bf16[3,12,3072,128]{3,2,1,0:T(8,128)(2,1)} %bitcast.20), custom_call_target="tpu_custom_call" | custom-call | flops 1769472 | bytes 7872 | tf_op jit(solution)/shard_map/input_terms/pallas_call | solution.py:334
  132.5 8.9 %collective-permute-done.16 = bf16[256,2304]{1,0:T(8,128)(2,1)S(1)} collective-permute-done((bf16[256,2304]{1,0:T(8,128)(2,1)S(1)}, bf16[256,2304]{1,0:T(8,128)(2,1)S(1)}, u32[]{:S(2)}, u32[]{:S(2)}) %collective-permute-start.16) | collective-permute-done | bytes 1179680 | tf_op jit(solution)/shard_map/ppermute | solution.py:553
  144.8 8.9 %output_terms.1 = (f32[256,1536]{1,0:T(8,128)}, bf16[256,1536]{1,0:T(8,128)(2,1)}) custom-call(s32[6]{0:T(128)} %stack.23.place_ref, bf16[256,768]{1,0:T(8,128)(2,1)} %get-tuple-element.56.own_ref, bf16[256,768]{1,0:T(8,128)(2,1)} %copy-done.13, bf16[1536,3072]{1,0:T(8,128)(2,1)} %bitcast.21, bf16[1536,3072]{1,0:T(8,128)(2,1)} %bitcast.22), custom_call_target="tpu_custom_call" | custom-call | flops 589824 | bytes 3072 | tf_op jit(solution)/shard_map/output_terms/pallas_call | solution.py:511
  158.6 16.6 %collective-permute-done.21 = bf16[256,2304]{1,0:T(8,128)(2,1)} collective-permute-done((bf16[256,2304]{1,0:T(8,128)(2,1)S(1)}, bf16[256,2304]{1,0:T(8,128)(2,1)}, u32[]{:S(2)}, u32[]{:S(2)}) %collective-permute-start.21) | collective-permute-done | bytes 1179680 | tf_op jit(solution)/shard_map/ppermute | solution.py:553
  175.2 2.5 %select_select_fusion.1.refs_3_ = bf16[256,2304]{1,0:T(8,128)(2,1)} fusion(bf16[256,2304]{1,0:T(8,128)(2,1)} %collective-permute-done.20, bf16[256,2304]{1,0:T(8,128)(2,1)S(1)} %collective-permute-done.17, bf16[256,2304]{1,0:T(8,128)(2,1)S(1)} %collective-permute-done.16, bf16[256,2304]{1,0:T(8,128)(2,1)} %collective-permute-done.21, pred[]{:T(512)S(6)} %eq.21, ...), kind=kLoop, calls=%fused_computation.14 | loop fusion | flops 1769472 | bytes 5898243 | tf_op jit(solution)/shard_map/jit(_where)/select_n | solution.py:589
  184.4 2.5 %collective-permute-start.26 = (bf16[256,384]{1,0:T(8,128)(2,1)}, bf16[256,384]{1,0:T(8,128)(2,1)S(1)}, u32[]{:S(2)}, u32[]{:S(2)}) collective-permute-start(bf16[256,384]{1,0:T(8,128)(2,1)} %get-tuple-element.110), channel_id=1, source_target_pairs={{0,3},{1,0},{2,1},{3,2},{4,7},{5,4},{6,5},{7,6},{8,11},{9,8},{10,9... | collective-permute-start | bytes 589832 | tf_op jit(solution)/shard_map/ppermute | solution.py:600
  186.9 8.9 %weight_terms.2.refs_4_ = bf16[3,12,768,128]{3,2,1,0:T(8,128)(2,1)} custom-call(s32[6]{0:T(128)} %stack.23.place_ref, bf16[1024,768]{1,0:T(8,128)(2,1)} %maximum_select_fusion.3.x_ref, bf16[256,2304]{1,0:T(8,128)(2,1)} %get-tuple-element.55.d_own_ref.refs_0_, bf16[256,2304]{1,0:T(8,128)(2,1)} %copy-done.5, bf16[256,2304]{1,0:T(8,128)(2,1)} %copy-done.4, ...), custom_call_target="tpu_custom_call" | custom-call | flops 884736 | bytes 2400 | tf_op jit(solution)/shard_map/weight_terms/pallas_call | solution.py:393
  195.8 9.6 %collective-permute-done.26 = bf16[256,384]{1,0:T(8,128)(2,1)S(1)} collective-permute-done((bf16[256,384]{1,0:T(8,128)(2,1)}, bf16[256,384]{1,0:T(8,128)(2,1)S(1)}, u32[]{:S(2)}, u32[]{:S(2)}) %collective-permute-start.26) | collective-permute-done | bytes 196640 | tf_op jit(solution)/shard_map/ppermute | solution.py:600
  207.8 12.3 %collective-permute-done.27 = bf16[256,384]{1,0:T(8,128)(2,1)S(1)} collective-permute-done((bf16[256,384]{1,0:T(8,128)(2,1)S(1)}, bf16[256,384]{1,0:T(8,128)(2,1)S(1)}, u32[]{:S(2)}, u32[]{:S(2)}) %collective-permute-start.27) | collective-permute-done | bytes 196640 | tf_op jit(solution)/shard_map/ppermute | solution.py:600
  222.1 8.8 %weight_terms.3 = bf16[3,12,768,128]{3,2,1,0:T(8,128)(2,1)} custom-call(s32[6]{0:T(128)} %stack.23.place_ref, bf16[1024,768]{1,0:T(8,128)(2,1)} %maximum_select_fusion.3.x_ref, bf16[256,2304]{1,0:T(8,128)(2,1)} %copy-done.6, bf16[256,2304]{1,0:T(8,128)(2,1)} %collective-permute-done.18.refs_1_, ...), custom_call_target="tpu_custom_call", output_to_operand_aliasing={{}: (6, {})} | custom-call | flops 884736 | bytes 2400 | tf_op jit(solution)/shard_map/weight_terms/pallas_call | solution.py:393
  233.4 8.3 %out_terms.1 = bf16[384,3072]{1,0:T(8,128)(2,1)} custom-call(s32[6]{0:T(128)} %stack.23.place_ref, bf16[1024,384]{1,0:T(8,128)(2,1)} %pad_maximum_fusion.2.att_ref, bf16[256,1536]{1,0:T(8,128)(2,1)} %refs_0_.1, bf16[768,1536]{1,0:T(8,128)(2,1)} %copy-done, bf16[256,1536]{1,0:T(8,128)(2,1)} %copy-done.18, bf16[768,1536]{1,0:T(8,128)(2,1)} %copy-done.8), custom_call_target="tpu_custom_call" | custom-call | flops 589824 | bytes 2304 | tf_op jit(solution)/shard_map/out_terms/pallas_call | solution.py:453
  (117 shorter events, 43.0 us)
Async XLA Ops:
  1.1 22.9 %collective-permute-start.4 = (bf16[256,1536]{1,0:T(8,128)(2,1)}, bf16[256,1536]{1,0:T(8,128)(2,1)S(1)}, u32[]{:S(2)}, u32[]{:S(2)}) collective-permute-start(bf16[256,1536]{1,0:T(8,128)(2,1)} %refs_0_.1), channel_id=1, source_target_pairs={{1,0},{2,1},{3,2},{5,4},{6,5},{7,6},{9,8},{10,9},{11,10},{13,12},{... | collective-permute-start | bytes 2359304 | tf_op jit(solution)/shard_map/ppermute | solution.py:553
  2.4 22.9 %collective-permute-start.6 = (bf16[256,1536]{1,0:T(8,128)(2,1)}, bf16[256,1536]{1,0:T(8,128)(2,1)S(1)}, u32[]{:S(2)}, u32[]{:S(2)}) collective-permute-start(bf16[256,1536]{1,0:T(8,128)(2,1)} %refs_0_.1), channel_id=1, source_target_pairs={{0,1},{1,2},{2,3},{4,5},{5,6},{6,7},{8,9},{9,10},{10,11},{12,13},{... | collective-permute-start | bytes 2359304 | tf_op jit(solution)/shard_map/ppermute | solution.py:554
  7.6 18.4 %collective-permute-start.2 = (bf16[256,1536]{1,0:T(8,128)(2,1)}, bf16[256,1536]{1,0:T(8,128)(2,1)S(1)}, u32[]{:S(2)}, u32[]{:S(2)}) collective-permute-start(bf16[256,1536]{1,0:T(8,128)(2,1)} %refs_0_.1), channel_id=1, source_target_pairs={{0,4},{4,0},{8,12},{12,8},{1,5},{5,1},{9,13},{13,9},{2,6},{6,2},{1... | collective-permute-start | bytes 2359304 | tf_op jit(solution)/shard_map/ppermute | solution.py:20
  19.0 39.9 %collective-permute-start.1 = (bf16[256,2304]{1,0:T(8,128)(2,1)}, bf16[256,2304]{1,0:T(8,128)(2,1)S(1)}, u32[]{:S(2)}, u32[]{:S(2)}) collective-permute-start(bf16[256,2304]{1,0:T(8,128)(2,1)} %project.3), channel_id=1, source_target_pairs={{0,8},{4,12},{8,0},{12,4},{1,9},{5,13},{9,1},{13,5},{2,10},{6,14},... | collective-permute-start | bytes 3538952 | tf_op jit(solution)/shard_map/ppermute | solution.py:20
  24.0 44.7 %collective-permute-start.5 = (bf16[256,1536]{1,0:T(8,128)(2,1)S(1)}, bf16[256,1536]{1,0:T(8,128)(2,1)}, u32[]{:S(2)}, u32[]{:S(2)}) collective-permute-start(bf16[256,1536]{1,0:T(8,128)(2,1)S(1)} %collective-permute-done.4), channel_id=1, source_target_pairs={{1,0},{2,1},{5,4},{6,5},{9,8},{10,9},{13,12},{14,13},{17,16},{18,1... | collective-permute-start | bytes 2359304 | tf_op jit(solution)/shard_map/ppermute | solution.py:553
  25.3 43.4 %collective-permute-start.7 = (bf16[256,1536]{1,0:T(8,128)(2,1)S(1)}, bf16[256,1536]{1,0:T(8,128)(2,1)S(1)}, u32[]{:S(2)}, u32[]{:S(2)}) collective-permute-start(bf16[256,1536]{1,0:T(8,128)(2,1)S(1)} %collective-permute-done.6), channel_id=1, source_target_pairs={{1,2},{2,3},{5,6},{6,7},{9,10},{10,11},{13,14},{14,15},{17,18},{18... | collective-permute-start | bytes 2359304 | tf_op jit(solution)/shard_map/ppermute | solution.py:554
  32.8 23.3 %collective-permute-start.3 = (bf16[256,768]{1,0:T(8,128)(2,1)S(1)}, bf16[256,768]{1,0:T(8,128)(2,1)S(1)}, u32[]{:S(2)}, u32[]{:S(2)}) collective-permute-start(bf16[256,768]{1,0:T(8,128)(2,1)S(1)} %dynamic-slice_convert_fusion), channel_id=1, source_target_pairs={{0,8},{4,12},{8,0},{12,4},{1,9},{5,13},{9,1},{13,5},{2,10},{6,14},... | collective-permute-start | bytes 1179656 | tf_op jit(solution)/shard_map/ppermute | solution.py:20
  35.0 40.0 %collective-permute-start.11 = (bf16[256,384]{1,0:T(8,128)(2,1)S(1)}, bf16[256,384]{1,0:T(8,128)(2,1)S(1)}, u32[]{:S(2)}, u32[]{:S(2)}) collective-permute-start(bf16[256,384]{1,0:T(8,128)(2,1)S(1)} %get-tuple-element.107), channel_id=1, source_target_pairs={{0,3},{1,0},{2,1},{3,2},{4,7},{5,4},{6,5},{7,6},{8,11},{9,8},{10,9... | collective-permute-start | bytes 589832 | tf_op jit(solution)/shard_map/ppermute | solution.py:600
  56.1 19.0 %collective-permute-start.12 = (bf16[256,384]{1,0:T(8,128)(2,1)S(1)}, bf16[256,384]{1,0:T(8,128)(2,1)S(1)}, u32[]{:S(2)}, u32[]{:S(2)}) collective-permute-start(bf16[256,384]{1,0:T(8,128)(2,1)S(1)} %get-tuple-element.106), channel_id=1, source_target_pairs={{0,2},{1,3},{2,0},{3,1},{4,6},{5,7},{6,4},{7,5},{8,10},{9,11},{10,... | collective-permute-start | bytes 589832 | tf_op jit(solution)/shard_map/ppermute | solution.py:600
  68.8 29.4 %collective-permute-start.8 = (bf16[256,2304]{1,0:T(8,128)(2,1)}, bf16[256,2304]{1,0:T(8,128)(2,1)S(1)}, u32[]{:S(2)}, u32[]{:S(2)}) collective-permute-start(bf16[256,2304]{1,0:T(8,128)(2,1)} %get-tuple-element.55.d_own_ref.refs_0_), channel_id=1, source_target_pairs={{1,0},{2,1},{3,2},{5,4},{6,5},{7,6},{9,8},{10,9},{11,10},{13,12},{... | collective-permute-start | bytes 3538952 | tf_op jit(solution)/shard_map/ppermute | solution.py:553
  70.2 29.2 %collective-permute-start.9 = (bf16[256,2304]{1,0:T(8,128)(2,1)}, bf16[256,2304]{1,0:T(8,128)(2,1)S(1)}, u32[]{:S(2)}, u32[]{:S(2)}) collective-permute-start(bf16[256,2304]{1,0:T(8,128)(2,1)} %get-tuple-element.55.d_own_ref.refs_0_), channel_id=1, source_target_pairs={{0,1},{1,2},{2,3},{4,5},{5,6},{6,7},{8,9},{9,10},{10,11},{12,13},{... | collective-permute-start | bytes 3538952 | tf_op jit(solution)/shard_map/ppermute | solution.py:554
  75.2 36.8 %collective-permute-start.10 = (bf16[256,2304]{1,0:T(8,128)(2,1)S(1)}, bf16[256,2304]{1,0:T(8,128)(2,1)S(1)}, u32[]{:S(2)}, u32[]{:S(2)}) collective-permute-start(bf16[256,2304]{1,0:T(8,128)(2,1)S(1)} %copy-done.7), channel_id=1, source_target_pairs={{0,8},{4,12},{8,0},{12,4},{1,9},{5,13},{9,1},{13,5},{2,10},{6,14},... | collective-permute-start | bytes 3538952 | tf_op jit(solution)/shard_map/ppermute | solution.py:20
  87.5 24.6 %collective-permute-start.15 = (bf16[256,768]{1,0:T(8,128)(2,1)S(1)}, bf16[256,768]{1,0:T(8,128)(2,1)S(1)}, u32[]{:S(2)}, u32[]{:S(2)}) collective-permute-start(bf16[256,768]{1,0:T(8,128)(2,1)S(1)} %copy-done.11), channel_id=1, source_target_pairs={{0,8},{4,12},{8,0},{12,4},{1,9},{5,13},{9,1},{13,5},{2,10},{6,14},... | collective-permute-start | bytes 1179656 | tf_op jit(solution)/shard_map/ppermute | solution.py:20
  112.0 29.4 %collective-permute-start.16 = (bf16[256,2304]{1,0:T(8,128)(2,1)S(1)}, bf16[256,2304]{1,0:T(8,128)(2,1)S(1)}, u32[]{:S(2)}, u32[]{:S(2)}) collective-permute-start(bf16[256,2304]{1,0:T(8,128)(2,1)S(1)} %collective-permute-done.8), channel_id=1, source_target_pairs={{1,0},{2,1},{5,4},{6,5},{9,8},{10,9},{13,12},{14,13},{17,16},{18,1... | collective-permute-start | bytes 3538952 | tf_op jit(solution)/shard_map/ppermute | solution.py:553
  113.4 28.1 %collective-permute-start.17 = (bf16[256,2304]{1,0:T(8,128)(2,1)S(1)}, bf16[256,2304]{1,0:T(8,128)(2,1)S(1)}, u32[]{:S(2)}, u32[]{:S(2)}) collective-permute-start(bf16[256,2304]{1,0:T(8,128)(2,1)S(1)} %collective-permute-done.9), channel_id=1, source_target_pairs={{1,2},{2,3},{5,6},{6,7},{9,10},{10,11},{13,14},{14,15},{17,18},{18... | collective-permute-start | bytes 3538952 | tf_op jit(solution)/shard_map/ppermute | solution.py:554
  114.1 27.7 %collective-permute-start.18 = (bf16[256,2304]{1,0:T(8,128)(2,1)S(1)}, bf16[256,2304]{1,0:T(8,128)(2,1)}, u32[]{:S(2)}, u32[]{:S(2)}) collective-permute-start(bf16[256,2304]{1,0:T(8,128)(2,1)S(1)} %select_select_fusion.refs_1_), channel_id=1, source_target_pairs={{0,8},{4,12},{8,0},{12,4},{1,9},{5,13},{9,1},{13,5},{2,10},{6,14},... | collective-permute-start | bytes 3538952 | tf_op jit(solution)/shard_map/ppermute | solution.py:20
  141.8 16.8 %collective-permute-start.20 = (bf16[256,2304]{1,0:T(8,128)(2,1)S(1)}, bf16[256,2304]{1,0:T(8,128)(2,1)}, u32[]{:S(2)}, u32[]{:S(2)}) collective-permute-start(bf16[256,2304]{1,0:T(8,128)(2,1)S(1)} %collective-permute-done.17), channel_id=1, source_target_pairs={{2,3},{6,7},{10,11},{14,15},{18,19},{22,23},{26,27},{30,31}} | collective-permute-start | bytes 3538952 | tf_op jit(solution)/shard_map/ppermute | solution.py:554
  143.5 31.7 %collective-permute-start.21 = (bf16[256,2304]{1,0:T(8,128)(2,1)S(1)}, bf16[256,2304]{1,0:T(8,128)(2,1)}, u32[]{:S(2)}, u32[]{:S(2)}) collective-permute-start(bf16[256,2304]{1,0:T(8,128)(2,1)S(1)} %collective-permute-done.16), channel_id=1, source_target_pairs={{1,0},{5,4},{9,8},{13,12},{17,16},{21,20},{25,24},{29,28}} | collective-permute-start | bytes 3538952 | tf_op jit(solution)/shard_map/ppermute | solution.py:553
  154.8 29.5 %collective-permute-start.19 = (bf16[256,2304]{1,0:T(8,128)(2,1)S(1)}, bf16[256,2304]{1,0:T(8,128)(2,1)}, u32[]{:S(2)}, u32[]{:S(2)}) collective-permute-start(bf16[256,2304]{1,0:T(8,128)(2,1)S(1)} %select_select_fusion.2.refs_2_), channel_id=1, source_target_pairs={{0,8},{4,12},{8,0},{12,4},{1,9},{5,13},{9,1},{13,5},{2,10},{6,14},... | collective-permute-start | bytes 3538952 | tf_op jit(solution)/shard_map/ppermute | solution.py:20
  177.7 27.7 %collective-permute-start.29 = (bf16[256,1536]{1,0:T(8,128)(2,1)}, bf16[256,1536]{1,0:T(8,128)(2,1)}, u32[]{:S(2)}, u32[]{:S(2)}) collective-permute-start(bf16[256,1536]{1,0:T(8,128)(2,1)} %get-tuple-element.85), channel_id=1, source_target_pairs={{0,4},{4,0},{8,12},{12,8},{1,5},{5,1},{9,13},{13,9},{2,6},{6,2},{1... | collective-permute-start | bytes 2359304 | tf_op jit(solution)/shard_map/ppermute | solution.py:20
  177.7 42.4 %collective-permute-start.23 = (bf16[256,2304]{1,0:T(8,128)(2,1)}, bf16[256,2304]{1,0:T(8,128)(2,1)S(1)}, u32[]{:S(2)}, u32[]{:S(2)}) collective-permute-start(bf16[256,2304]{1,0:T(8,128)(2,1)} %select_select_fusion.1.refs_3_), channel_id=1, source_target_pairs={{0,8},{4,12},{8,0},{12,4},{1,9},{5,13},{9,1},{13,5},{2,10},{6,14},... | collective-permute-start | bytes 3538952 | tf_op jit(solution)/shard_map/ppermute | solution.py:20
  179.5 40.6 %collective-permute-start.24 = (bf16[256,1536]{1,0:T(8,128)(2,1)}, bf16[256,1536]{1,0:T(8,128)(2,1)S(1)}, u32[]{:S(2)}, u32[]{:S(2)}) collective-permute-start(bf16[256,1536]{1,0:T(8,128)(2,1)} %collective-permute-done.5), channel_id=1, source_target_pairs={{1,0},{5,4},{9,8},{13,12},{17,16},{21,20},{25,24},{29,28}} | collective-permute-start | bytes 2359304 | tf_op jit(solution)/shard_map/ppermute | solution.py:553
  180.7 39.3 %collective-permute-start.25 = (bf16[256,1536]{1,0:T(8,128)(2,1)}, bf16[256,1536]{1,0:T(8,128)(2,1)}, u32[]{:S(2)}, u32[]{:S(2)}) collective-permute-start(bf16[256,1536]{1,0:T(8,128)(2,1)} %copy-done.23), channel_id=1, source_target_pairs={{2,3},{6,7},{10,11},{14,15},{18,19},{22,23},{26,27},{30,31}} | collective-permute-start | bytes 2359304 | tf_op jit(solution)/shard_map/ppermute | solution.py:554
  184.4 21.1 %collective-permute-start.26 = (bf16[256,384]{1,0:T(8,128)(2,1)}, bf16[256,384]{1,0:T(8,128)(2,1)S(1)}, u32[]{:S(2)}, u32[]{:S(2)}) collective-permute-start(bf16[256,384]{1,0:T(8,128)(2,1)} %get-tuple-element.110), channel_id=1, source_target_pairs={{0,3},{1,0},{2,1},{3,2},{4,7},{5,4},{6,5},{7,6},{8,11},{9,8},{10,9... | collective-permute-start | bytes 589832 | tf_op jit(solution)/shard_map/ppermute | solution.py:600
  (33 other events, 338.1 us)
where the time goes:
time: 243 us; the launch traced here: 242 us
  waiting for transfers between devices  80.6 us (33%)
  Pallas kernels  79.7 us (33%)
  starting transfers between devices  45.6 us (19%)
  other arithmetic  22.6 us (9%)
  matrix products  6.6 us (3%)
  local copies, waits for them, and re-layouts  5.51 us (2%)
    ppermute x6, waiting for transfers between devices, line_step(): lax.ppermute(upper[-1], axis, [(d + 1, d) for d in range(count - step)])  37.8 us
    ppermute x6, waiting for transfers between devices, send_slots(): slots.append(lax.ppermute(blocks_of(target), axis, pairs))  21.9 us
    ppermute x13, waiting for transfers between devices, partner_2(): return lax.ppermute(value, axis, pairs)  19.7 us
    pallas_call x2, Pallas kernels, project(): pl.pallas_call(proj_kernel, grid_spec=pltpu.PrefetchScalarGridSpec(num_sc...  19.1 us
    pallas_call x2, Pallas kernels, weight_terms(): pl.pallas_call(functools.partial(weight_kernel, count), grid_spec=pltpu.P...  17.8 us
    pallas_call x1, Pallas kernels, input_terms(): pl.pallas_call(input_kernel, grid_spec=pltpu.PrefetchScalarGridSpec(num_s...  16.8 us
    ppermute x6, starting transfers between devices, line_step(): lax.ppermute(lower[-1], axis, [(d - 1, d) for d in range(step, count)])  14.7 us
    ppermute x13, starting transfers between devices, partner_2(): return lax.ppermute(value, axis, pairs)  12.6 us
  transfers between devices with their start and end apart: 31, of which 11 were waited for; matrix products, arithmetic and copies ran while one was open for 13% of the time, Pallas kernels for 30%

commit v1 on v0

--- a/solution.py
+++ b/solution.py
@@ -361,16 +361,21 @@
     )(place, d_own, d_other, weights, weights)
 
 
-def weight_kernel(count, place_ref, x_ref, *refs):
+def weight_kernel(count, place_ref, x_own_ref, x_other_ref, *refs):
     slots, out_ref, x_sorted = refs[:count], refs[-2], refs[-1]
     heads, head_dim = out_ref.shape[1], out_ref.shape[3]
-    patches = x_ref.shape[0] // count
+    patches, part_rows = x_own_ref.shape[0] // count, x_own_ref.shape[1]
 
     @pl.when(pl.program_id(0) == 0)
     def _():
-        for slot in range(count):
-            offset = pl.multiple_of(place_ref[2 + slot] * patches, patches)
-            x_sorted[:, slot * patches : (slot + 1) * patches] = x_ref[pl.ds(offset, patches), :].T
+        for side, x_ref in enumerate((x_own_ref, x_other_ref)):
+            first = (place_ref[1] + side) % 2 * part_rows
+            rows = pl.ds(pl.multiple_of(first, part_rows), part_rows)
+            for slot in range(count):
+                offset = pl.multiple_of(place_ref[2 + slot] * patches, patches)
+                x_sorted[rows, slot * patches : (slot + 1) * patches] = x_ref[
+                    pl.ds(offset, patches), :
+                ].T
 
     grads = jnp.concatenate([slot_ref[...] for slot_ref in slots], axis=0)
     total = jnp.dot(x_sorted[...], grads, preferred_element_type=jnp.float32)
@@ -380,10 +385,10 @@
             out_ref[part, head] = total[:, column : column + head_dim].astype(out_ref.dtype)
 
 
-def weight_terms(place, x_slots, slots, swap, start, shape, filled):
+def weight_terms(place, x_own, x_other, slots, swap, start, shape, filled):
     count = len(slots)
-    rows, width = slots[0].shape
-    block_rows = x_slots.shape[1]
+    rows, width = slots[-1].shape
+    block_rows = 2 * x_own.shape[1]
     head_dim = shape[3]
     heads = width // (3 * head_dim)
     group = 2 if heads % 2 == 0 and start % 2 == 0 else 1
@@ -395,7 +400,7 @@
         grid_spec=pltpu.PrefetchScalarGridSpec(
             num_scalar_prefetch=1,
             grid=(heads // group,),
-            in_specs=[pl.BlockSpec(x_slots.shape, lambda step, place: (0, 0))]
+            in_specs=[pl.BlockSpec(x_own.shape, lambda step, place: (0, 0))] * 2
             + [part] * count
             + [pl.BlockSpec(memory_space=pl.ANY)] * len(filled),
             out_specs=pl.BlockSpec(
@@ -407,18 +412,18 @@
                     0,
                 ),
             ),
-            scratch_shapes=[pltpu.VMEM(x_slots.shape[::-1], x_slots.dtype)],
+            scratch_shapes=[pltpu.VMEM((block_rows, x_own.shape[0]), x_own.dtype)],
         ),
         out_shape=jax.ShapeDtypeStruct(shape, jnp.bfloat16),
-        input_output_aliases={2 + count: 0} if filled else {},
+        input_output_aliases={3 + count: 0} if filled else {},
         compiler_params=params("arbitrary"),
-        cost_estimate=hint(
+        cost_estimate=pl.CostEstimate(
             flops=2 * count * rows * block_rows * width,
             bytes_accessed=2 * count * rows * (block_rows + width) + 2 * block_rows * width,
             transcendentals=0,
         ),
         name="weight_terms",
-    )(place, x_slots, *slots, *filled)
+    )(place, x_own, x_other, *slots, *filled)
 
 
 def out_kernel(count, place_ref, att_ref, *refs):
@@ -505,6 +510,7 @@
 
 def output_terms(place, att_own, att_other, w_back):
     rows, half = att_own.shape
+    last = att_other.shape[1] // half - 1
     piece = w_back.shape[1] // 2
     whole = pl.BlockSpec((rows, half), lambda step, place: (0, 0))
     result = pl.BlockSpec((rows, piece), lambda step, place: (0, 0))
@@ -515,7 +521,7 @@
             grid=(2,),
             in_specs=[
                 whole,
-                whole,
+                pl.BlockSpec((rows, half), lambda step, place: (0, last)),
                 pl.BlockSpec(
                     (half, piece), lambda step, place: (place[0], (place[1] + 1 + step) % 2)
                 ),
@@ -658,26 +664,27 @@
         d_proj.append(parts[1])
     attended, d_proj = jnp.concatenate(attended, axis=1), jnp.concatenate(d_proj, axis=1)
 
-    d_proj, g_line = together(d_proj, g_line)
+    d_proj, attended, g_line, x_parts = together(d_proj, attended, g_line, x_parts)
     upper, lower = [d_proj], [d_proj]
-    own, other = [d_proj], [y_swap(d_proj)]
-    attended_other = y_swap(attended)
+    own, other = [d_proj], [y_swap(jnp.concatenate([d_proj, attended], axis=1))]
 
     line_step(upper, lower, "depth")
     slot = pick_arrival(upper, lower, 0, table, "depth")
-    x_part = jnp.concatenate(x_parts, axis=0)
-    x_slots = ordered(col_place, x_part, core_swap(x_part), 1)
-    upper, lower, slot, other, x_slots, attended_other = together(
-        upper, lower, slot, other, x_slots, attended_other
-    )
+    x_own = jnp.concatenate(x_parts, axis=0)
+    x_swapped = core_swap(x_own)
+    upper, lower, slot, other, x_own, x_swapped, attended = together(
+        upper, lower, slot, other, x_own, x_swapped, attended
+    )
+    attended_panel = ordered(row_place, attended, other[0][:, d_proj.shape[1] :], 1)
     own.append(slot)
     other.append(y_swap(slot))
 
     line_step(upper, lower, "depth")
     slot = pick_arrival(upper, lower, 1, table, "depth")
     input_keep, input_send = input_terms(place, own[0], other[0], weights)
-    upper, lower, slot, other, input_keep, input_send = together(
-        upper, lower, slot, other, input_keep, input_send
+    out_keep, out_send = output_terms(place, attended, other[0], w_back)
+    upper, lower, slot, other, input_keep, input_send, out_keep, out_send, attended_panel = together(
+        upper, lower, slot, other, input_keep, input_send, out_keep, out_send, attended_panel
     )
     own.append(slot)
     other.append(y_swap(slot))
@@ -685,10 +692,9 @@
     line_step(upper, lower, "depth")
     input_grad = (input_keep + core_swap(input_send).astype(jnp.float32)).astype(low)
     slot = pick_arrival(upper, lower, 2, table, "depth")
-    attended_panel = ordered(row_place, attended, attended_other, 1)
-    out_keep, out_send = output_terms(place, attended, attended_other, w_back)
-    slot, x_slots, input_grad, attended_panel, g_line, out_keep, out_send = together(
-        slot, x_slots, input_grad, attended_panel, g_line, out_keep, out_send
+    attention_out = (out_keep + core_swap(out_send).astype(jnp.float32)).astype(low)
+    slot, x_own, input_grad, attended_panel, g_line = together(
+        slot, x_own, input_grad, attended_panel, g_line
     )
     own.append(slot)
     other.append(y_swap(slot))
@@ -701,15 +707,14 @@
         ),
         "depth",
     )
-    attention_out = (out_keep + core_swap(out_send).astype(jnp.float32)).astype(low)
-    filled = weight_terms(place, x_slots, own, 0, 0, shape, None)
+    filled = weight_terms(place, x_own, x_swapped, own, 0, 0, shape, None)
     other, g_line, a_slots, attention_out, filled = together(
         other, g_line, a_slots, attention_out, filled
     )
 
     g_far = jnp.concatenate(by_offset(*g_line, "depth"), axis=0)
     g_far_other = core_swap(g_far)
-    filled = weight_terms(place, x_slots, other, 1, 0, shape, filled)
+    filled = weight_terms(place, x_own, x_swapped, other, 1, 0, shape, filled)
     out_proj_grad = out_terms(
         place,
         jnp.concatenate(a_slots, axis=0),

time: 243 us -> 236 us (0.971)
  other arithmetic: 22.6 us -> 14.5 us
  waiting for transfers between devices: 80.6 us -> 85.7 us
    ppermute x6, waiting for transfers between devices: 37.8 us -> 61.9 us  [line_step(): lax.ppermute(upper[-1], axis, [(d + 1, d) for d in range(count - step)])]
    ppermute x6, waiting for transfers between devices: 21.9 us -> 7.5 us  [send_slots(): slots.append(lax.ppermute(blocks_of(target), axis, pairs))]
    select_n x3 -> x2, other arithmetic: 11.4 us -> 0.57 us  [ordered(): jnp.where(place == 0, jnp.concatenate([own, other], along), jnp.concatena...]
    ppermute x13 -> x12, waiting for transfers between devices: 19.7 us -> 15.1 us  [partner_2(): return lax.ppermute(value, axis, pairs)]
    ppermute x13 -> x12, starting transfers between devices: 12.6 us -> 9.33 us  [partner_2(): return lax.ppermute(value, axis, pairs)]
    ppermute x6, starting transfers between devices: 10.5 us -> 13.3 us  [send_slots(): slots.append(lax.ppermute(blocks_of(target), axis, pairs))]
    select_n x3, other arithmetic: 2.83 us -> 5.48 us  [pick_arrival(): jnp.where(place == other, source, picked)]
  transfers between devices with their start and end apart: 31 -> 30, of which waited for: 11 -> 9; matrix products, arithmetic and copies ran while one was open for 13% -> 9% of each run, Pallas kernels for 30% -> 30%
where the time goes in v1:
time: 236 us; the launch traced here: 235 us
  waiting for transfers between devices  85.7 us (36%)
  Pallas kernels  78.2 us (33%)
  starting transfers between devices  46 us (19%)
  other arithmetic  14.5 us (6%)
  matrix products  6.6 us (3%)
  local copies, waits for them, and re-layouts  3.39 us (1%)
    ppermute x6, waiting for transfers between devices, line_step(): lax.ppermute(upper[-1], axis, [(d + 1, d) for d in range(count - step)])  61.9 us
    pallas_call x2, Pallas kernels, project(): pl.pallas_call(proj_kernel, grid_spec=pltpu.PrefetchScalarGridSpec(num_sc...  19.1 us
    pallas_call x2, Pallas kernels, weight_terms(): pl.pallas_call(functools.partial(weight_kernel, count), grid_spec=pltpu.P...  17.5 us
    pallas_call x1, Pallas kernels, input_terms(): pl.pallas_call(input_kernel, grid_spec=pltpu.PrefetchScalarGridSpec(num_s...  17 us
    ppermute x6, starting transfers between devices, line_step(): lax.ppermute(lower[-1], axis, [(d - 1, d) for d in range(step, count)])  15.6 us
    ppermute x12, waiting for transfers between devices, partner_2(): return lax.ppermute(value, axis, pairs)  15.1 us
    ppermute x6, starting transfers between devices, send_slots(): slots.append(lax.ppermute(blocks_of(target), axis, pairs))  13.3 us
    ppermute x12, starting transfers between devices, partner_2(): return lax.ppermute(value, axis, pairs)  9.33 us
  transfers between devices with their start and end apart: 30, of which 9 were waited for; matrix products, arithmetic and copies ran while one was open for 9% of the time, Pallas kernels for 30%

profile of v1, /device:TPU:0, one launch (start us, length us, event | category | flops | bytes accessed | tf_op | source)
XLA Modules:
  0.0 235.3 jit_solution(11209880652207933034)
XLA Ops:
  2.4 5.2 %collective-permute-start.6 = (bf16[256,1536]{1,0:T(8,128)(2,1)}, bf16[256,1536]{1,0:T(8,128)(2,1)S(1)}, u32[]{:S(2)}, u32[]{:S(2)}) collective-permute-start(bf16[256,1536]{1,0:T(8,128)(2,1)} %refs_0_.1), channel_id=1, source_target_pairs={{0,1},{1,2},{2,3},{4,5},{5,6},{6,7},{8,9},{9,10},{10,11},{12,13},{... | collective-permute-start | bytes 2359304 | tf_op jit(solution)/shard_map/ppermute | solution.py:560
  9.4 9.5 %project.3 = bf16[256,2304]{1,0:T(8,128)(2,1)} custom-call(s32[6]{0:T(128)} %stack.23.place_ref, bf16[256,1536]{1,0:T(8,128)(2,1)} %own_ref.3, bf16[256,1536]{1,0:T(8,128)(2,1)} %copy-done.3, bf16[3,12,3072,128]{3,2,1,0:T(8,128)(2,1)} %bitcast.15, bf16[3,12,3072,128]{3,2,1,0:T(8,128)(2,1)} %bitcast.16), custom_call_target="tpu_custom_call" | custom-call | flops 884736 | bytes 4416 | tf_op jit(solution)/shard_map/project/pallas_call | solution.py:211
  20.9 3.3 %collective-permute-done.4 = bf16[256,1536]{1,0:T(8,128)(2,1)} collective-permute-done((bf16[256,1536]{1,0:T(8,128)(2,1)}, bf16[256,1536]{1,0:T(8,128)(2,1)}, u32[]{:S(2)}, u32[]{:S(2)}) %collective-permute-start.4) | collective-permute-done | bytes 786464 | tf_op jit(solution)/shard_map/ppermute | solution.py:559
  27.1 6.6 %fusion = f32[256,1536]{1,0:T(8,128)S(1)} fusion(bf16[256,1536]{1,0:T(8,128)(2,1)S(1)} %collective-permute-done.2.refs_2_, bf16[256,1536]{1,0:T(8,128)(2,1)S(1)} %copy-done.12, pred[]{:T(512)S(6)} %eq.24, bf16[1,1536,3072]{2,1,0:T(8,128)(2,1)} %param.6), kind=kOutput, calls=%fused_computation.3 | convolution fusion | flops 2422996992 | bytes 12582913 | tf_op jit(solution)/shard_map/dot_general | solution.py:61
  36.0 5.6 %collective-permute-start.10 = (bf16[256,384]{1,0:T(8,128)(2,1)S(1)}, bf16[256,384]{1,0:T(8,128)(2,1)S(1)}, u32[]{:S(2)}, u32[]{:S(2)}) collective-permute-start(bf16[256,384]{1,0:T(8,128)(2,1)S(1)} %get-tuple-element.118), channel_id=1, source_target_pairs={{0,1},{1,2},{2,3},{3,0},{4,5},{5,6},{6,7},{7,4},{8,9},{9,10},{10,1... | collective-permute-start | bytes 589832 | tf_op jit(solution)/shard_map/ppermute | solution.py:606
  41.6 9.6 %project.2.keep_ref = f32[256,2304]{1,0:T(8,128)} custom-call(s32[6]{0:T(128)} %stack.23.place_ref, bf16[256,1536]{1,0:T(8,128)(2,1)} %own_ref.3, bf16[256,1536]{1,0:T(8,128)(2,1)} %copy-done.3, bf16[3,12,3072,128]{3,2,1,0:T(8,128)(2,1)} %bitcast.17, bf16[3,12,3072,128]{3,2,1,0:T(8,128)(2,1)} %bitcast.18), custom_call_target="tpu_custom_call" | custom-call | flops 884736 | bytes 4416 | tf_op jit(solution)/shard_map/project/pallas_call | solution.py:211
  51.2 4.8 %collective-permute-done.3 = bf16[256,768]{1,0:T(8,128)(2,1)S(1)} collective-permute-done((bf16[256,768]{1,0:T(8,128)(2,1)S(1)}, bf16[256,768]{1,0:T(8,128)(2,1)S(1)}, u32[]{:S(2)}, u32[]{:S(2)}) %collective-permute-start.3) | collective-permute-done | bytes 393248 | tf_op jit(solution)/shard_map/ppermute | solution.py:20
  56.0 2.4 %collective-permute-start.8 = (bf16[256,384]{1,0:T(8,128)(2,1)S(1)}, bf16[256,384]{1,0:T(8,128)(2,1)S(1)}, u32[]{:S(2)}, u32[]{:S(2)}) collective-permute-start(bf16[256,384]{1,0:T(8,128)(2,1)S(1)} %get-tuple-element.120), channel_id=1, source_target_pairs={{0,3},{1,0},{2,1},{3,2},{4,7},{5,4},{6,5},{7,6},{8,11},{9,8},{10,9... | collective-permute-start | bytes 589832 | tf_op jit(solution)/shard_map/ppermute | solution.py:606
  60.5 8.7 %attend.1 = (bf16[256,768]{1,0:T(8,128)(2,1)}, bf16[256,2304]{1,0:T(8,128)(2,1)}) custom-call(f32[256,2304]{1,0:T(8,128)} %project.2.keep_ref, bf16[256,2304]{1,0:T(8,128)(2,1)} %copy-done.10, bf16[256,768]{1,0:T(8,128)(2,1)} %add_convert_fusion.2.d_out_ref), custom_call_target="tpu_custom_call" | custom-call | flops 172032 | bytes 1344 | tf_op jit(solution)/shard_map/attend/pallas_call | solution.py:271
  69.3 3.4 %collective-permute-done.9 = bf16[256,384]{1,0:T(8,128)(2,1)S(1)} collective-permute-done((bf16[256,384]{1,0:T(8,128)(2,1)S(1)}, bf16[256,384]{1,0:T(8,128)(2,1)S(1)}, u32[]{:S(2)}, u32[]{:S(2)}) %collective-permute-start.9) | collective-permute-done | bytes 196640 | tf_op jit(solution)/shard_map/ppermute | solution.py:606
  74.0 5.6 %collective-permute-start.12 = (bf16[256,2304]{1,0:T(8,128)(2,1)}, bf16[256,2304]{1,0:T(8,128)(2,1)}, u32[]{:S(2)}, u32[]{:S(2)}) collective-permute-start(bf16[256,2304]{1,0:T(8,128)(2,1)} %get-tuple-element.63.d_own_ref.refs_0_), channel_id=1, source_target_pairs={{0,1},{1,2},{2,3},{4,5},{5,6},{6,7},{8,9},{9,10},{10,11},{12,13},{... | collective-permute-start | bytes 3538952 | tf_op jit(solution)/shard_map/ppermute | solution.py:560
  83.0 18.7 %collective-permute-done.11 = bf16[256,2304]{1,0:T(8,128)(2,1)} collective-permute-done((bf16[256,2304]{1,0:T(8,128)(2,1)}, bf16[256,2304]{1,0:T(8,128)(2,1)}, u32[]{:S(2)}, u32[]{:S(2)}) %collective-permute-start.11) | collective-permute-done | bytes 1179680 | tf_op jit(solution)/shard_map/ppermute | solution.py:559
  102.9 2.8 %select_select_fusion.refs_1_ = bf16[256,2304]{1,0:T(8,128)(2,1)} fusion(bf16[256,2304]{1,0:T(8,128)(2,1)} %collective-permute-done.12, bf16[256,2304]{1,0:T(8,128)(2,1)} %collective-permute-done.11, pred[]{:T(512)S(6)} %eq.22, pred[]{:T(512)S(6)} %eq.23), kind=kLoop, calls=%fused_computation.1 | loop fusion | flops 1179648 | bytes 3538946 | tf_op jit(solution)/shard_map/jit(_where)/select_n | solution.py:595
  105.7 10.3 %collective-permute-done.13.d_other_ref.other_ref.refs_0_ = bf16[256,3072]{1,0:T(8,128)(2,1)S(1)} collective-permute-done((bf16[256,3072]{1,0:T(8,128)(2,1)S(1)}, bf16[256,3072]{1,0:T(8,128)(2,1)S(1)}, u32[]{:S(2)}, u32[]{:S(2)}) %collective-permute-start.13) | collective-permute-done | bytes 1572896 | tf_op jit(solution)/shard_map/ppermute | solution.py:20
  120.5 7.6 %output_terms.1 = (f32[256,1536]{1,0:T(8,128)}, bf16[256,1536]{1,0:T(8,128)(2,1)}) custom-call(s32[6]{0:T(128)} %stack.23.place_ref, bf16[256,768]{1,0:T(8,128)(2,1)} %get-tuple-element.75.own_ref, bf16[256,3072]{1,0:T(8,128)(2,1)} %copy-done, bf16[1536,3072]{1,0:T(8,128)(2,1)} %bitcast.21, bf16[1536,3072]{1,0:T(8,128)(2,1)} %bitcast.22), custom_call_target="tpu_custom_call" | custom-call | flops 589824 | bytes 3072 | tf_op jit(solution)/shard_map/output_terms/pallas_call | solution.py:517
  128.1 17.0 %input_terms.1 = (f32[256,1536]{1,0:T(8,128)}, bf16[256,1536]{1,0:T(8,128)(2,1)}) custom-call(s32[6]{0:T(128)} %stack.23.place_ref, bf16[256,2304]{1,0:T(8,128)(2,1)} %get-tuple-element.63.d_own_ref.refs_0_, bf16[256,3072]{1,0:T(8,128)(2,1)} %copy-done, bf16[3,12,3072,128]{3,2,1,0:T(8,128)(2,1)} %bitcast.19, bf16[3,12,3072,128]{3,2,1,0:T(8,128)(2,1)} %bitcast.20), custom_call_target="tpu_custom_call" | custom-call | flops 1769472 | bytes 7872 | tf_op jit(solution)/shard_map/input_terms/pallas_call | solution.py:334
  150.8 29.3 %collective-permute-done.20 = bf16[256,2304]{1,0:T(8,128)(2,1)S(1)} collective-permute-done((bf16[256,2304]{1,0:T(8,128)(2,1)S(1)}, bf16[256,2304]{1,0:T(8,128)(2,1)S(1)}, u32[]{:S(2)}, u32[]{:S(2)}) %collective-permute-start.20) | collective-permute-done | bytes 1179680 | tf_op jit(solution)/shard_map/ppermute | solution.py:559
  185.6 2.2 add_convert_fusion
  187.8 2.2 collective-permute-start.26
  190.6 8.7 %weight_terms.2.refs_4_ = bf16[3,12,768,128]{3,2,1,0:T(8,128)(2,1)} custom-call(s32[6]{0:T(128)} %stack.23.place_ref, bf16[1024,384]{1,0:T(8,128)(2,1)} %copy-done.9, bf16[1024,384]{1,0:T(8,128)(2,1)} %copy-done.11, bf16[256,2304]{1,0:T(8,128)(2,1)} %get-tuple-element.63.d_own_ref.refs_0_, bf16[256,2304]{1,0:T(8,128)(2,1)} %select_select_fusion.refs_1_, ...), custom_call_target="tpu_custom_call" | custom-call | flops 3623878656 | bytes 9830400 | tf_op jit(solution)/shard_map/weight_terms/pallas_call | solution.py:398
  199.3 4.0 %collective-permute-done.26 = bf16[256,384]{1,0:T(8,128)(2,1)S(1)} collective-permute-done((bf16[256,384]{1,0:T(8,128)(2,1)S(1)}, bf16[256,384]{1,0:T(8,128)(2,1)S(1)}, u32[]{:S(2)}, u32[]{:S(2)}) %collective-permute-start.26) | collective-permute-done | bytes 196640 | tf_op jit(solution)/shard_map/ppermute | solution.py:606
  203.4 10.6 %collective-permute-done.23 = bf16[256,1536]{1,0:T(8,128)(2,1)S(1)} collective-permute-done((bf16[256,1536]{1,0:T(8,128)(2,1)S(1)}, bf16[256,1536]{1,0:T(8,128)(2,1)S(1)}, u32[]{:S(2)}, u32[]{:S(2)}) %collective-permute-start.23) | collective-permute-done | bytes 786464 | tf_op jit(solution)/shard_map/ppermute | solution.py:559
  216.8 8.7 %weight_terms.3 = bf16[3,12,768,128]{3,2,1,0:T(8,128)(2,1)} custom-call(s32[6]{0:T(128)} %stack.23.place_ref, bf16[1024,384]{1,0:T(8,128)(2,1)} %copy-done.9, bf16[1024,384]{1,0:T(8,128)(2,1)} %copy-done.11, bf16[256,3072]{1,0:T(8,128)(2,1)} %copy-done, bf16[256,2304]{1,0:T(8,128)(2,1)} %collective-permute-done.17.refs_1_, ...), custom_call_target="tpu_custom_call", output_to_operand_aliasing={{}: (7, {})} | custom-call | flops 3623878656 | bytes 9830400 | tf_op jit(solution)/shard_map/weight_terms/pallas_call | solution.py:398
  227.1 8.3 %out_terms.1 = bf16[384,3072]{1,0:T(8,128)(2,1)} custom-call(s32[6]{0:T(128)} %stack.23.place_ref, bf16[1024,384]{1,0:T(8,128)(2,1)} %pad_maximum_fusion.2.att_ref, bf16[256,1536]{1,0:T(8,128)(2,1)} %refs_0_.1, bf16[768,1536]{1,0:T(8,128)(2,1)} %copy-done.1, bf16[256,1536]{1,0:T(8,128)(2,1)} %copy-done.13, bf16[768,1536]{1,0:T(8,128)(2,1)} %copy-done.6), custom_call_target="tpu_custom_call" | custom-call | flops 589824 | bytes 2304 | tf_op jit(solution)/shard_map/out_terms/pallas_call | solution.py:458
  (106 shorter events, 39.1 us)
Async XLA Ops:
  1.1 23.0 %collective-permute-start.4 = (bf16[256,1536]{1,0:T(8,128)(2,1)}, bf16[256,1536]{1,0:T(8,128)(2,1)}, u32[]{:S(2)}, u32[]{:S(2)}) collective-permute-start(bf16[256,1536]{1,0:T(8,128)(2,1)} %refs_0_.1), channel_id=1, source_target_pairs={{1,0},{2,1},{3,2},{5,4},{6,5},{7,6},{9,8},{10,9},{11,10},{13,12},{... | collective-permute-start | bytes 2359304 | tf_op jit(solution)/shard_map/ppermute | solution.py:559
  2.4 23.0 %collective-permute-start.6 = (bf16[256,1536]{1,0:T(8,128)(2,1)}, bf16[256,1536]{1,0:T(8,128)(2,1)S(1)}, u32[]{:S(2)}, u32[]{:S(2)}) collective-permute-start(bf16[256,1536]{1,0:T(8,128)(2,1)} %refs_0_.1), channel_id=1, source_target_pairs={{0,1},{1,2},{2,3},{4,5},{5,6},{6,7},{8,9},{9,10},{10,11},{12,13},{... | collective-permute-start | bytes 2359304 | tf_op jit(solution)/shard_map/ppermute | solution.py:560
  7.6 19.4 %collective-permute-start.2 = (bf16[256,1536]{1,0:T(8,128)(2,1)}, bf16[256,1536]{1,0:T(8,128)(2,1)S(1)}, u32[]{:S(2)}, u32[]{:S(2)}) collective-permute-start(bf16[256,1536]{1,0:T(8,128)(2,1)} %refs_0_.1), channel_id=1, source_target_pairs={{0,4},{4,0},{8,12},{12,8},{1,5},{5,1},{9,13},{13,9},{2,6},{6,2},{1... | collective-permute-start | bytes 2359304 | tf_op jit(solution)/shard_map/ppermute | solution.py:20
  18.9 39.5 %collective-permute-start.1 = (bf16[256,2304]{1,0:T(8,128)(2,1)}, bf16[256,2304]{1,0:T(8,128)(2,1)S(1)}, u32[]{:S(2)}, u32[]{:S(2)}) collective-permute-start(bf16[256,2304]{1,0:T(8,128)(2,1)} %project.3), channel_id=1, source_target_pairs={{0,8},{4,12},{8,0},{12,4},{1,9},{5,13},{9,1},{13,5},{2,10},{6,14},... | collective-permute-start | bytes 3538952 | tf_op jit(solution)/shard_map/ppermute | solution.py:20
  24.1 48.5 %collective-permute-start.5 = (bf16[256,1536]{1,0:T(8,128)(2,1)}, bf16[256,1536]{1,0:T(8,128)(2,1)S(1)}, u32[]{:S(2)}, u32[]{:S(2)}) collective-permute-start(bf16[256,1536]{1,0:T(8,128)(2,1)} %collective-permute-done.4), channel_id=1, source_target_pairs={{1,0},{2,1},{5,4},{6,5},{9,8},{10,9},{13,12},{14,13},{17,16},{18,1... | collective-permute-start | bytes 2359304 | tf_op jit(solution)/shard_map/ppermute | solution.py:559
  25.5 47.2 %collective-permute-start.7 = (bf16[256,1536]{1,0:T(8,128)(2,1)S(1)}, bf16[256,1536]{1,0:T(8,128)(2,1)}, u32[]{:S(2)}, u32[]{:S(2)}) collective-permute-start(bf16[256,1536]{1,0:T(8,128)(2,1)S(1)} %collective-permute-done.6), channel_id=1, source_target_pairs={{1,2},{2,3},{5,6},{6,7},{9,10},{10,11},{13,14},{14,15},{17,18},{18... | collective-permute-start | bytes 2359304 | tf_op jit(solution)/shard_map/ppermute | solution.py:560
  33.7 22.3 %collective-permute-start.3 = (bf16[256,768]{1,0:T(8,128)(2,1)S(1)}, bf16[256,768]{1,0:T(8,128)(2,1)S(1)}, u32[]{:S(2)}, u32[]{:S(2)}) collective-permute-start(bf16[256,768]{1,0:T(8,128)(2,1)S(1)} %dynamic-slice_convert_fusion), channel_id=1, source_target_pairs={{0,8},{4,12},{8,0},{12,4},{1,9},{5,13},{9,1},{13,5},{2,10},{6,14},... | collective-permute-start | bytes 1179656 | tf_op jit(solution)/shard_map/ppermute | solution.py:20
  36.0 33.2 %collective-permute-start.10 = (bf16[256,384]{1,0:T(8,128)(2,1)S(1)}, bf16[256,384]{1,0:T(8,128)(2,1)S(1)}, u32[]{:S(2)}, u32[]{:S(2)}) collective-permute-start(bf16[256,384]{1,0:T(8,128)(2,1)S(1)} %get-tuple-element.118), channel_id=1, source_target_pairs={{0,1},{1,2},{2,3},{3,0},{4,5},{5,6},{6,7},{7,4},{8,9},{9,10},{10,1... | collective-permute-start | bytes 589832 | tf_op jit(solution)/shard_map/ppermute | solution.py:606
  58.4 14.2 %collective-permute-start.9 = (bf16[256,384]{1,0:T(8,128)(2,1)S(1)}, bf16[256,384]{1,0:T(8,128)(2,1)S(1)}, u32[]{:S(2)}, u32[]{:S(2)}) collective-permute-start(bf16[256,384]{1,0:T(8,128)(2,1)S(1)} %get-tuple-element.119), channel_id=1, source_target_pairs={{0,2},{1,3},{2,0},{3,1},{4,6},{5,7},{6,4},{7,5},{8,10},{9,11},{10,... | collective-permute-start | bytes 589832 | tf_op jit(solution)/shard_map/ppermute | solution.py:606
  72.7 29.0 %collective-permute-start.11 = (bf16[256,2304]{1,0:T(8,128)(2,1)}, bf16[256,2304]{1,0:T(8,128)(2,1)}, u32[]{:S(2)}, u32[]{:S(2)}) collective-permute-start(bf16[256,2304]{1,0:T(8,128)(2,1)} %get-tuple-element.63.d_own_ref.refs_0_), channel_id=1, source_target_pairs={{1,0},{2,1},{3,2},{5,4},{6,5},{7,6},{9,8},{10,9},{11,10},{13,12},{... | collective-permute-start | bytes 3538952 | tf_op jit(solution)/shard_map/ppermute | solution.py:559
  74.0 28.9 %collective-permute-start.12 = (bf16[256,2304]{1,0:T(8,128)(2,1)}, bf16[256,2304]{1,0:T(8,128)(2,1)}, u32[]{:S(2)}, u32[]{:S(2)}) collective-permute-start(bf16[256,2304]{1,0:T(8,128)(2,1)} %get-tuple-element.63.d_own_ref.refs_0_), channel_id=1, source_target_pairs={{0,1},{1,2},{2,3},{4,5},{5,6},{6,7},{8,9},{9,10},{10,11},{12,13},{... | collective-permute-start | bytes 3538952 | tf_op jit(solution)/shard_map/ppermute | solution.py:560
  81.2 34.8 %collective-permute-start.13 = (bf16[256,3072]{1,0:T(8,128)(2,1)S(1)}, bf16[256,3072]{1,0:T(8,128)(2,1)S(1)}, u32[]{:S(2)}, u32[]{:S(2)}) collective-permute-start(bf16[256,3072]{1,0:T(8,128)(2,1)S(1)} %pad_maximum_fusion.1), channel_id=1, source_target_pairs={{0,8},{4,12},{8,0},{12,4},{1,9},{5,13},{9,1},{13,5},{2,10},{6,14},... | collective-permute-start | bytes 4718600 | tf_op jit(solution)/shard_map/ppermute | solution.py:20
  82.9 22.7 %collective-permute-start.14 = (bf16[1024,384]{1,0:T(8,128)(2,1)S(1)}, bf16[1024,384]{1,0:T(8,128)(2,1)S(1)}, u32[]{:S(2)}, u32[]{:S(2)}) collective-permute-start(bf16[1024,384]{1,0:T(8,128)(2,1)S(1)} %constant_dynamic-update-slice_fusion.x_own_ref), channel_id=1, source_target_pairs={{0,4},{4,0},{8,12},{12,8},{1,5},{5,1},{9,13},{13,9},{2,6},{6,2},{1... | collective-permute-start | bytes 2359304 | tf_op jit(solution)/shard_map/ppermute | solution.py:20
  115.9 29.4 %collective-permute-start.15 = (bf16[256,2304]{1,0:T(8,128)(2,1)}, bf16[256,2304]{1,0:T(8,128)(2,1)S(1)}, u32[]{:S(2)}, u32[]{:S(2)}) collective-permute-start(bf16[256,2304]{1,0:T(8,128)(2,1)} %collective-permute-done.11), channel_id=1, source_target_pairs={{1,0},{2,1},{5,4},{6,5},{9,8},{10,9},{13,12},{14,13},{17,16},{18,1... | collective-permute-start | bytes 3538952 | tf_op jit(solution)/shard_map/ppermute | solution.py:559
  117.2 28.1 %collective-permute-start.16 = (bf16[256,2304]{1,0:T(8,128)(2,1)}, bf16[256,2304]{1,0:T(8,128)(2,1)}, u32[]{:S(2)}, u32[]{:S(2)}) collective-permute-start(bf16[256,2304]{1,0:T(8,128)(2,1)} %collective-permute-done.12), channel_id=1, source_target_pairs={{1,2},{2,3},{5,6},{6,7},{9,10},{10,11},{13,14},{14,15},{17,18},{18... | collective-permute-start | bytes 3538952 | tf_op jit(solution)/shard_map/ppermute | solution.py:560
  119.0 27.6 %collective-permute-start.17 = (bf16[256,2304]{1,0:T(8,128)(2,1)}, bf16[256,2304]{1,0:T(8,128)(2,1)}, u32[]{:S(2)}, u32[]{:S(2)}) collective-permute-start(bf16[256,2304]{1,0:T(8,128)(2,1)} %select_select_fusion.refs_1_), channel_id=1, source_target_pairs={{0,8},{4,12},{8,0},{12,4},{1,9},{5,13},{9,1},{13,5},{2,10},{6,14},... | collective-permute-start | bytes 3538952 | tf_op jit(solution)/shard_map/ppermute | solution.py:20
  147.3 32.8 %collective-permute-start.20 = (bf16[256,2304]{1,0:T(8,128)(2,1)S(1)}, bf16[256,2304]{1,0:T(8,128)(2,1)S(1)}, u32[]{:S(2)}, u32[]{:S(2)}) collective-permute-start(bf16[256,2304]{1,0:T(8,128)(2,1)S(1)} %collective-permute-done.15), channel_id=1, source_target_pairs={{1,0},{5,4},{9,8},{13,12},{17,16},{21,20},{25,24},{29,28}} | collective-permute-start | bytes 3538952 | tf_op jit(solution)/shard_map/ppermute | solution.py:559
  148.6 36.2 %collective-permute-start.28 = (bf16[256,1536]{1,0:T(8,128)(2,1)}, bf16[256,1536]{1,0:T(8,128)(2,1)}, u32[]{:S(2)}, u32[]{:S(2)}) collective-permute-start(bf16[256,1536]{1,0:T(8,128)(2,1)} %get-tuple-element.98), channel_id=1, source_target_pairs={{0,4},{4,0},{8,12},{12,8},{1,5},{5,1},{9,13},{13,9},{2,6},{6,2},{1... | collective-permute-start | bytes 2359304 | tf_op jit(solution)/shard_map/ppermute | solution.py:20
  149.2 38.6 %collective-permute-start.18 = (bf16[256,2304]{1,0:T(8,128)(2,1)}, bf16[256,2304]{1,0:T(8,128)(2,1)}, u32[]{:S(2)}, u32[]{:S(2)}) collective-permute-start(bf16[256,2304]{1,0:T(8,128)(2,1)} %select_select_fusion.2.refs_2_), channel_id=1, source_target_pairs={{0,8},{4,12},{8,0},{12,4},{1,9},{5,13},{9,1},{13,5},{2,10},{6,14},... | collective-permute-start | bytes 3538952 | tf_op jit(solution)/shard_map/ppermute | solution.py:20
  181.6 32.4 %collective-permute-start.22 = (bf16[256,2304]{1,0:T(8,128)(2,1)}, bf16[256,2304]{1,0:T(8,128)(2,1)}, u32[]{:S(2)}, u32[]{:S(2)}) collective-permute-start(bf16[256,2304]{1,0:T(8,128)(2,1)} %select_select_fusion.1.refs_3_), channel_id=1, source_target_pairs={{0,8},{4,12},{8,0},{12,4},{1,9},{5,13},{9,1},{13,5},{2,10},{6,14},... | collective-permute-start | bytes 3538952 | tf_op jit(solution)/shard_map/ppermute | solution.py:20
  183.6 30.4 %collective-permute-start.23 = (bf16[256,1536]{1,0:T(8,128)(2,1)S(1)}, bf16[256,1536]{1,0:T(8,128)(2,1)S(1)}, u32[]{:S(2)}, u32[]{:S(2)}) collective-permute-start(bf16[256,1536]{1,0:T(8,128)(2,1)S(1)} %copy-done.17), channel_id=1, source_target_pairs={{1,0},{5,4},{9,8},{13,12},{17,16},{21,20},{25,24},{29,28}} | collective-permute-start | bytes 2359304 | tf_op jit(solution)/shard_map/ppermute | solution.py:559
  184.9 29.1 %collective-permute-start.24 = (bf16[256,1536]{1,0:T(8,128)(2,1)}, bf16[256,1536]{1,0:T(8,128)(2,1)S(1)}, u32[]{:S(2)}, u32[]{:S(2)}) collective-permute-start(bf16[256,1536]{1,0:T(8,128)(2,1)} %collective-permute-done.7), channel_id=1, source_target_pairs={{2,3},{6,7},{10,11},{14,15},{18,19},{22,23},{26,27},{30,31}} | collective-permute-start | bytes 2359304 | tf_op jit(solution)/shard_map/ppermute | solution.py:560
  187.8 15.5 %collective-permute-start.26 = (bf16[256,384]{1,0:T(8,128)(2,1)S(1)}, bf16[256,384]{1,0:T(8,128)(2,1)S(1)}, u32[]{:S(2)}, u32[]{:S(2)}) collective-permute-start(bf16[256,384]{1,0:T(8,128)(2,1)S(1)} %get-tuple-element.123), channel_id=1, source_target_pairs={{0,2},{1,3},{2,0},{3,1},{4,6},{5,7},{6,4},{7,5},{8,10},{9,11},{10,... | collective-permute-start | bytes 589832 | tf_op jit(solution)/shard_map/ppermute | solution.py:606
  190.1 13.3 %collective-permute-start.27 = (bf16[256,384]{1,0:T(8,128)(2,1)S(1)}, bf16[256,384]{1,0:T(8,128)(2,1)S(1)}, u32[]{:S(2)}, u32[]{:S(2)}) collective-permute-start(bf16[256,384]{1,0:T(8,128)(2,1)S(1)} %get-tuple-element.122), channel_id=1, source_target_pairs={{0,1},{1,2},{2,3},{3,0},{4,5},{5,6},{6,7},{7,4},{8,9},{9,10},{10,1... | collective-permute-start | bytes 589832 | tf_op jit(solution)/shard_map/ppermute | solution.py:606
  (26 other events, 234.0 us)

commit v2 on v1

--- a/solution.py
+++ b/solution.py
@@ -708,13 +708,12 @@
         "depth",
     )
     filled = weight_terms(place, x_own, x_swapped, own, 0, 0, shape, None)
-    other, g_line, a_slots, attention_out, filled = together(
-        other, g_line, a_slots, attention_out, filled
-    )
-
+    other, attention_out, filled = together(other, attention_out, filled)
+
+    filled = weight_terms(place, x_own, x_swapped, other, 1, 0, shape, filled)
+    g_line, a_slots, filled = together(g_line, a_slots, filled)
     g_far = jnp.concatenate(by_offset(*g_line, "depth"), axis=0)
     g_far_other = core_swap(g_far)
-    filled = weight_terms(place, x_own, x_swapped, other, 1, 0, shape, filled)
     out_proj_grad = out_terms(
         place,
         jnp.concatenate(a_slots, axis=0),

time: 236 us -> 237 us (level)
  waiting for transfers between devices: 85.7 us -> 83.3 us
    ppermute x12, waiting for transfers between devices: 15.1 us -> 27.5 us  [partner_2(): return lax.ppermute(value, axis, pairs)]
    ppermute x6, waiting for transfers between devices: 61.9 us -> 51.3 us  [line_step(): lax.ppermute(upper[-1], axis, [(d + 1, d) for d in range(count - step)])]
    ppermute x6, waiting for transfers between devices: 7.5 us -> 3.42 us  [send_slots(): slots.append(lax.ppermute(blocks_of(target), axis, pairs))]
where the time goes in v2:
time: 237 us; the launch traced here: 236 us
  waiting for transfers between devices  83.3 us (35%)
  Pallas kernels  78.2 us (33%)
  starting transfers between devices  46.2 us (19%)
  other arithmetic  14.8 us (6%)
  matrix products  6.6 us (3%)
  local copies, waits for them, and re-layouts  5.42 us (2%)
    ppermute x6, waiting for transfers between devices, line_step(): lax.ppermute(upper[-1], axis, [(d + 1, d) for d in range(count - step)])  51.3 us
    ppermute x12, waiting for transfers between devices, partner_2(): return lax.ppermute(value, axis, pairs)  27.5 us
    pallas_call x2, Pallas kernels, project(): pl.pallas_call(proj_kernel, grid_spec=pltpu.PrefetchScalarGridSpec(num_sc...  19.1 us
    pallas_call x2, Pallas kernels, weight_terms(): pl.pallas_call(functools.partial(weight_kernel, count), grid_spec=pltpu.P...  17.5 us
    pallas_call x1, Pallas kernels, input_terms(): pl.pallas_call(input_kernel, grid_spec=pltpu.PrefetchScalarGridSpec(num_s...  17 us
    ppermute x6, starting transfers between devices, line_step(): lax.ppermute(lower[-1], axis, [(d - 1, d) for d in range(step, count)])  15.7 us
    ppermute x6, starting transfers between devices, send_slots(): slots.append(lax.ppermute(blocks_of(target), axis, pairs))  13.5 us
    ppermute x12, starting transfers between devices, partner_2(): return lax.ppermute(value, axis, pairs)  9.19 us
  transfers between devices with their start and end apart: 30, of which 9 were waited for; matrix products, arithmetic and copies ran while one was open for 9% of the time, Pallas kernels for 30%

profile of v2, /device:TPU:0, one launch (start us, length us, event | category | flops | bytes accessed | tf_op | source)
XLA Modules:
  0.0 235.5 jit_solution(11238914247160333085)
XLA Ops:
  2.4 5.2 %collective-permute-start.6 = (bf16[256,1536]{1,0:T(8,128)(2,1)}, bf16[256,1536]{1,0:T(8,128)(2,1)S(1)}, u32[]{:S(2)}, u32[]{:S(2)}) collective-permute-start(bf16[256,1536]{1,0:T(8,128)(2,1)} %refs_0_.1), channel_id=1, source_target_pairs={{0,1},{1,2},{2,3},{4,5},{5,6},{6,7},{8,9},{9,10},{10,11},{12,13},{... | collective-permute-start | bytes 2359304 | tf_op jit(solution)/shard_map/ppermute | solution.py:560
  9.4 9.5 %project.3 = bf16[256,2304]{1,0:T(8,128)(2,1)} custom-call(s32[6]{0:T(128)} %stack.23.place_ref, bf16[256,1536]{1,0:T(8,128)(2,1)} %own_ref.3, bf16[256,1536]{1,0:T(8,128)(2,1)} %copy-done.3, bf16[3,12,3072,128]{3,2,1,0:T(8,128)(2,1)} %bitcast.15, bf16[3,12,3072,128]{3,2,1,0:T(8,128)(2,1)} %bitcast.16), custom_call_target="tpu_custom_call" | custom-call | flops 884736 | bytes 4416 | tf_op jit(solution)/shard_map/project/pallas_call | solution.py:211
  20.9 3.2 %collective-permute-done.4 = bf16[256,1536]{1,0:T(8,128)(2,1)} collective-permute-done((bf16[256,1536]{1,0:T(8,128)(2,1)}, bf16[256,1536]{1,0:T(8,128)(2,1)}, u32[]{:S(2)}, u32[]{:S(2)}) %collective-permute-start.4) | collective-permute-done | bytes 786464 | tf_op jit(solution)/shard_map/ppermute | solution.py:559
  27.1 6.6 %fusion = f32[256,1536]{1,0:T(8,128)S(1)} fusion(bf16[256,1536]{1,0:T(8,128)(2,1)S(1)} %collective-permute-done.2.refs_2_, bf16[256,1536]{1,0:T(8,128)(2,1)S(1)} %copy-done.12, pred[]{:T(512)S(6)} %eq.24, bf16[1,1536,3072]{2,1,0:T(8,128)(2,1)} %param.6), kind=kOutput, calls=%fused_computation.3 | convolution fusion | flops 2422996992 | bytes 12582913 | tf_op jit(solution)/shard_map/dot_general | solution.py:61
  36.0 5.6 %collective-permute-start.10 = (bf16[256,384]{1,0:T(8,128)(2,1)S(1)}, bf16[256,384]{1,0:T(8,128)(2,1)S(1)}, u32[]{:S(2)}, u32[]{:S(2)}) collective-permute-start(bf16[256,384]{1,0:T(8,128)(2,1)S(1)} %get-tuple-element.120), channel_id=1, source_target_pairs={{0,1},{1,2},{2,3},{3,0},{4,5},{5,6},{6,7},{7,4},{8,9},{9,10},{10,1... | collective-permute-start | bytes 589832 | tf_op jit(solution)/shard_map/ppermute | solution.py:606
  41.6 9.6 %project.2.keep_ref = f32[256,2304]{1,0:T(8,128)} custom-call(s32[6]{0:T(128)} %stack.23.place_ref, bf16[256,1536]{1,0:T(8,128)(2,1)} %own_ref.3, bf16[256,1536]{1,0:T(8,128)(2,1)} %copy-done.3, bf16[3,12,3072,128]{3,2,1,0:T(8,128)(2,1)} %bitcast.17, bf16[3,12,3072,128]{3,2,1,0:T(8,128)(2,1)} %bitcast.18), custom_call_target="tpu_custom_call" | custom-call | flops 884736 | bytes 4416 | tf_op jit(solution)/shard_map/project/pallas_call | solution.py:211
  51.2 4.9 %collective-permute-done.3 = bf16[256,768]{1,0:T(8,128)(2,1)S(1)} collective-permute-done((bf16[256,768]{1,0:T(8,128)(2,1)S(1)}, bf16[256,768]{1,0:T(8,128)(2,1)S(1)}, u32[]{:S(2)}, u32[]{:S(2)}) %collective-permute-start.3) | collective-permute-done | bytes 393248 | tf_op jit(solution)/shard_map/ppermute | solution.py:20
  56.0 2.5 %collective-permute-start.8 = (bf16[256,384]{1,0:T(8,128)(2,1)S(1)}, bf16[256,384]{1,0:T(8,128)(2,1)S(1)}, u32[]{:S(2)}, u32[]{:S(2)}) collective-permute-start(bf16[256,384]{1,0:T(8,128)(2,1)S(1)} %get-tuple-element.122), channel_id=1, source_target_pairs={{0,3},{1,0},{2,1},{3,2},{4,7},{5,4},{6,5},{7,6},{8,11},{9,8},{10,9... | collective-permute-start | bytes 589832 | tf_op jit(solution)/shard_map/ppermute | solution.py:606
  60.6 8.7 %attend.1 = (bf16[256,768]{1,0:T(8,128)(2,1)}, bf16[256,2304]{1,0:T(8,128)(2,1)}) custom-call(f32[256,2304]{1,0:T(8,128)} %project.2.keep_ref, bf16[256,2304]{1,0:T(8,128)(2,1)} %copy-done.10, bf16[256,768]{1,0:T(8,128)(2,1)} %add_convert_fusion.2.d_out_ref), custom_call_target="tpu_custom_call" | custom-call | flops 172032 | bytes 1344 | tf_op jit(solution)/shard_map/attend/pallas_call | solution.py:271
  69.3 3.4 %collective-permute-done.9 = bf16[256,384]{1,0:T(8,128)(2,1)S(1)} collective-permute-done((bf16[256,384]{1,0:T(8,128)(2,1)S(1)}, bf16[256,384]{1,0:T(8,128)(2,1)S(1)}, u32[]{:S(2)}, u32[]{:S(2)}) %collective-permute-start.9) | collective-permute-done | bytes 196640 | tf_op jit(solution)/shard_map/ppermute | solution.py:606
  74.0 5.6 %collective-permute-start.12 = (bf16[256,2304]{1,0:T(8,128)(2,1)}, bf16[256,2304]{1,0:T(8,128)(2,1)}, u32[]{:S(2)}, u32[]{:S(2)}) collective-permute-start(bf16[256,2304]{1,0:T(8,128)(2,1)} %get-tuple-element.64.d_own_ref.refs_0_), channel_id=1, source_target_pairs={{0,1},{1,2},{2,3},{4,5},{5,6},{6,7},{8,9},{9,10},{10,11},{12,13},{... | collective-permute-start | bytes 3538952 | tf_op jit(solution)/shard_map/ppermute | solution.py:560
  83.0 18.7 %collective-permute-done.11 = bf16[256,2304]{1,0:T(8,128)(2,1)} collective-permute-done((bf16[256,2304]{1,0:T(8,128)(2,1)}, bf16[256,2304]{1,0:T(8,128)(2,1)}, u32[]{:S(2)}, u32[]{:S(2)}) %collective-permute-start.11) | collective-permute-done | bytes 1179680 | tf_op jit(solution)/shard_map/ppermute | solution.py:559
  102.9 2.8 %select_select_fusion.refs_1_ = bf16[256,2304]{1,0:T(8,128)(2,1)} fusion(bf16[256,2304]{1,0:T(8,128)(2,1)} %collective-permute-done.12, bf16[256,2304]{1,0:T(8,128)(2,1)} %collective-permute-done.11, pred[]{:T(512)S(6)} %eq.22, pred[]{:T(512)S(6)} %eq.23), kind=kLoop, calls=%fused_computation.1 | loop fusion | flops 1179648 | bytes 3538946 | tf_op jit(solution)/shard_map/jit(_where)/select_n | solution.py:595
  106.6 9.3 %collective-permute-done.13.d_other_ref.other_ref.refs_0_ = bf16[256,3072]{1,0:T(8,128)(2,1)S(1)} collective-permute-done((bf16[256,3072]{1,0:T(8,128)(2,1)S(1)}, bf16[256,3072]{1,0:T(8,128)(2,1)S(1)}, u32[]{:S(2)}, u32[]{:S(2)}) %collective-permute-start.13) | collective-permute-done | bytes 1572896 | tf_op jit(solution)/shard_map/ppermute | solution.py:20
  120.5 7.6 %output_terms.1 = (f32[256,1536]{1,0:T(8,128)}, bf16[256,1536]{1,0:T(8,128)(2,1)}) custom-call(s32[6]{0:T(128)} %stack.23.place_ref, bf16[256,768]{1,0:T(8,128)(2,1)} %get-tuple-element.76.own_ref, bf16[256,3072]{1,0:T(8,128)(2,1)} %copy-done, bf16[1536,3072]{1,0:T(8,128)(2,1)} %bitcast.21, bf16[1536,3072]{1,0:T(8,128)(2,1)} %bitcast.22), custom_call_target="tpu_custom_call" | custom-call | flops 589824 | bytes 3072 | tf_op jit(solution)/shard_map/output_terms/pallas_call | solution.py:517
  128.1 17.0 %input_terms.1 = (f32[256,1536]{1,0:T(8,128)}, bf16[256,1536]{1,0:T(8,128)(2,1)}) custom-call(s32[6]{0:T(128)} %stack.23.place_ref, bf16[256,2304]{1,0:T(8,128)(2,1)} %get-tuple-element.64.d_own_ref.refs_0_, bf16[256,3072]{1,0:T(8,128)(2,1)} %copy-done, bf16[3,12,3072,128]{3,2,1,0:T(8,128)(2,1)} %bitcast.19, bf16[3,12,3072,128]{3,2,1,0:T(8,128)(2,1)} %bitcast.20), custom_call_target="tpu_custom_call" | custom-call | flops 1769472 | bytes 7872 | tf_op jit(solution)/shard_map/input_terms/pallas_call | solution.py:334
  150.9 29.3 %collective-permute-done.20 = bf16[256,2304]{1,0:T(8,128)(2,1)S(1)} collective-permute-done((bf16[256,2304]{1,0:T(8,128)(2,1)S(1)}, bf16[256,2304]{1,0:T(8,128)(2,1)S(1)}, u32[]{:S(2)}, u32[]{:S(2)}) %collective-permute-start.20) | collective-permute-done | bytes 1179680 | tf_op jit(solution)/shard_map/ppermute | solution.py:559
  182.1 2.5 %add_convert_fusion = bf16[256,1536]{1,0:T(8,128)(2,1)} fusion(f32[256,1536]{1,0:T(8,128)} %get-tuple-element.93, bf16[256,1536]{1,0:T(8,128)(2,1)S(1)} %collective-permute-done.23), kind=kLoop, calls=%fused_computation.11 | loop fusion | flops 1179648 | bytes 3145728 | tf_op jit(solution)/shard_map/convert_element_type | solution.py:695
  188.2 8.7 %weight_terms.2.refs_4_ = bf16[3,12,768,128]{3,2,1,0:T(8,128)(2,1)} custom-call(s32[6]{0:T(128)} %stack.23.place_ref, bf16[1024,384]{1,0:T(8,128)(2,1)} %copy-done.8, bf16[1024,384]{1,0:T(8,128)(2,1)} %copy-done.11, bf16[256,2304]{1,0:T(8,128)(2,1)} %get-tuple-element.64.d_own_ref.refs_0_, bf16[256,2304]{1,0:T(8,128)(2,1)} %select_select_fusion.refs_1_, ...), custom_call_target="tpu_custom_call" | custom-call | flops 3623878656 | bytes 9830400 | tf_op jit(solution)/shard_map/weight_terms/pallas_call | solution.py:398
  196.9 2.9 %collective-permute-start.27 = (bf16[256,384]{1,0:T(8,128)(2,1)S(1)}, bf16[256,384]{1,0:T(8,128)(2,1)S(1)}, u32[]{:S(2)}, u32[]{:S(2)}) collective-permute-start(bf16[256,384]{1,0:T(8,128)(2,1)S(1)} %get-tuple-element.125), channel_id=1, source_target_pairs={{0,2},{1,3},{2,0},{3,1},{4,6},{5,7},{6,4},{7,5},{8,10},{9,11},{10,... | collective-permute-start | bytes 589832 | tf_op jit(solution)/shard_map/ppermute | solution.py:606
  199.8 9.8 %collective-permute-done.22.refs_3_ = bf16[256,2304]{1,0:T(8,128)(2,1)S(1)} collective-permute-done((bf16[256,2304]{1,0:T(8,128)(2,1)}, bf16[256,2304]{1,0:T(8,128)(2,1)S(1)}, u32[]{:S(2)}, u32[]{:S(2)}) %collective-permute-start.22) | collective-permute-done | bytes 1179680 | tf_op jit(solution)/shard_map/ppermute | solution.py:20
  210.7 8.7 %weight_terms.3 = bf16[3,12,768,128]{3,2,1,0:T(8,128)(2,1)} custom-call(s32[6]{0:T(128)} %stack.23.place_ref, bf16[1024,384]{1,0:T(8,128)(2,1)} %copy-done.8, bf16[1024,384]{1,0:T(8,128)(2,1)} %copy-done.11, bf16[256,3072]{1,0:T(8,128)(2,1)} %copy-done, bf16[256,2304]{1,0:T(8,128)(2,1)} %collective-permute-done.17.refs_1_, ...), custom_call_target="tpu_custom_call", output_to_operand_aliasing={{}: (7, {})} | custom-call | flops 3623878656 | bytes 9830400 | tf_op jit(solution)/shard_map/weight_terms/pallas_call | solution.py:398
  222.3 3.4 %collective-permute-done.29.refs_3_ = bf16[768,1536]{1,0:T(8,128)(2,1)S(1)} collective-permute-done((bf16[768,1536]{1,0:T(8,128)(2,1)S(1)}, bf16[768,1536]{1,0:T(8,128)(2,1)S(1)}, u32[]{:S(2)}, u32[]{:S(2)}) %collective-permute-start.29) | collective-permute-done | bytes 2359328 | tf_op jit(solution)/shard_map/ppermute | solution.py:20
  227.2 8.3 %out_terms.1 = bf16[384,3072]{1,0:T(8,128)(2,1)} custom-call(s32[6]{0:T(128)} %stack.23.place_ref, bf16[1024,384]{1,0:T(8,128)(2,1)} %pad_maximum_fusion.2.att_ref, bf16[256,1536]{1,0:T(8,128)(2,1)} %refs_0_.1, bf16[768,1536]{1,0:T(8,128)(2,1)} %copy-done.1, bf16[256,1536]{1,0:T(8,128)(2,1)} %copy-done.13, bf16[768,1536]{1,0:T(8,128)(2,1)} %copy-done.6), custom_call_target="tpu_custom_call" | custom-call | flops 589824 | bytes 2304 | tf_op jit(solution)/shard_map/out_terms/pallas_call | solution.py:458
  (108 shorter events, 40.6 us)
Async XLA Ops:
  1.1 23.0 %collective-permute-start.4 = (bf16[256,1536]{1,0:T(8,128)(2,1)}, bf16[256,1536]{1,0:T(8,128)(2,1)}, u32[]{:S(2)}, u32[]{:S(2)}) collective-permute-start(bf16[256,1536]{1,0:T(8,128)(2,1)} %refs_0_.1), channel_id=1, source_target_pairs={{1,0},{2,1},{3,2},{5,4},{6,5},{7,6},{9,8},{10,9},{11,10},{13,12},{... | collective-permute-start | bytes 2359304 | tf_op jit(solution)/shard_map/ppermute | solution.py:559
  2.4 23.0 %collective-permute-start.6 = (bf16[256,1536]{1,0:T(8,128)(2,1)}, bf16[256,1536]{1,0:T(8,128)(2,1)S(1)}, u32[]{:S(2)}, u32[]{:S(2)}) collective-permute-start(bf16[256,1536]{1,0:T(8,128)(2,1)} %refs_0_.1), channel_id=1, source_target_pairs={{0,1},{1,2},{2,3},{4,5},{5,6},{6,7},{8,9},{9,10},{10,11},{12,13},{... | collective-permute-start | bytes 2359304 | tf_op jit(solution)/shard_map/ppermute | solution.py:560
  7.6 19.4 %collective-permute-start.2 = (bf16[256,1536]{1,0:T(8,128)(2,1)}, bf16[256,1536]{1,0:T(8,128)(2,1)S(1)}, u32[]{:S(2)}, u32[]{:S(2)}) collective-permute-start(bf16[256,1536]{1,0:T(8,128)(2,1)} %refs_0_.1), channel_id=1, source_target_pairs={{0,4},{4,0},{8,12},{12,8},{1,5},{5,1},{9,13},{13,9},{2,6},{6,2},{1... | collective-permute-start | bytes 2359304 | tf_op jit(solution)/shard_map/ppermute | solution.py:20
  18.9 39.6 %collective-permute-start.1 = (bf16[256,2304]{1,0:T(8,128)(2,1)}, bf16[256,2304]{1,0:T(8,128)(2,1)S(1)}, u32[]{:S(2)}, u32[]{:S(2)}) collective-permute-start(bf16[256,2304]{1,0:T(8,128)(2,1)} %project.3), channel_id=1, source_target_pairs={{0,8},{4,12},{8,0},{12,4},{1,9},{5,13},{9,1},{13,5},{2,10},{6,14},... | collective-permute-start | bytes 3538952 | tf_op jit(solution)/shard_map/ppermute | solution.py:20
  24.1 48.6 %collective-permute-start.5 = (bf16[256,1536]{1,0:T(8,128)(2,1)}, bf16[256,1536]{1,0:T(8,128)(2,1)S(1)}, u32[]{:S(2)}, u32[]{:S(2)}) collective-permute-start(bf16[256,1536]{1,0:T(8,128)(2,1)} %collective-permute-done.4), channel_id=1, source_target_pairs={{1,0},{2,1},{5,4},{6,5},{9,8},{10,9},{13,12},{14,13},{17,16},{18,1... | collective-permute-start | bytes 2359304 | tf_op jit(solution)/shard_map/ppermute | solution.py:559
  25.5 47.3 %collective-permute-start.7 = (bf16[256,1536]{1,0:T(8,128)(2,1)S(1)}, bf16[256,1536]{1,0:T(8,128)(2,1)}, u32[]{:S(2)}, u32[]{:S(2)}) collective-permute-start(bf16[256,1536]{1,0:T(8,128)(2,1)S(1)} %collective-permute-done.6), channel_id=1, source_target_pairs={{1,2},{2,3},{5,6},{6,7},{9,10},{10,11},{13,14},{14,15},{17,18},{18... | collective-permute-start | bytes 2359304 | tf_op jit(solution)/shard_map/ppermute | solution.py:560
  33.7 22.3 %collective-permute-start.3 = (bf16[256,768]{1,0:T(8,128)(2,1)S(1)}, bf16[256,768]{1,0:T(8,128)(2,1)S(1)}, u32[]{:S(2)}, u32[]{:S(2)}) collective-permute-start(bf16[256,768]{1,0:T(8,128)(2,1)S(1)} %dynamic-slice_convert_fusion), channel_id=1, source_target_pairs={{0,8},{4,12},{8,0},{12,4},{1,9},{5,13},{9,1},{13,5},{2,10},{6,14},... | collective-permute-start | bytes 1179656 | tf_op jit(solution)/shard_map/ppermute | solution.py:20
  36.0 33.3 %collective-permute-start.10 = (bf16[256,384]{1,0:T(8,128)(2,1)S(1)}, bf16[256,384]{1,0:T(8,128)(2,1)S(1)}, u32[]{:S(2)}, u32[]{:S(2)}) collective-permute-start(bf16[256,384]{1,0:T(8,128)(2,1)S(1)} %get-tuple-element.120), channel_id=1, source_target_pairs={{0,1},{1,2},{2,3},{3,0},{4,5},{5,6},{6,7},{7,4},{8,9},{9,10},{10,1... | collective-permute-start | bytes 589832 | tf_op jit(solution)/shard_map/ppermute | solution.py:606
  58.5 14.2 %collective-permute-start.9 = (bf16[256,384]{1,0:T(8,128)(2,1)S(1)}, bf16[256,384]{1,0:T(8,128)(2,1)S(1)}, u32[]{:S(2)}, u32[]{:S(2)}) collective-permute-start(bf16[256,384]{1,0:T(8,128)(2,1)S(1)} %get-tuple-element.121), channel_id=1, source_target_pairs={{0,2},{1,3},{2,0},{3,1},{4,6},{5,7},{6,4},{7,5},{8,10},{9,11},{10,... | collective-permute-start | bytes 589832 | tf_op jit(solution)/shard_map/ppermute | solution.py:606
  72.7 29.0 %collective-permute-start.11 = (bf16[256,2304]{1,0:T(8,128)(2,1)}, bf16[256,2304]{1,0:T(8,128)(2,1)}, u32[]{:S(2)}, u32[]{:S(2)}) collective-permute-start(bf16[256,2304]{1,0:T(8,128)(2,1)} %get-tuple-element.64.d_own_ref.refs_0_), channel_id=1, source_target_pairs={{1,0},{2,1},{3,2},{5,4},{6,5},{7,6},{9,8},{10,9},{11,10},{13,12},{... | collective-permute-start | bytes 3538952 | tf_op jit(solution)/shard_map/ppermute | solution.py:559
  74.0 28.9 %collective-permute-start.12 = (bf16[256,2304]{1,0:T(8,128)(2,1)}, bf16[256,2304]{1,0:T(8,128)(2,1)}, u32[]{:S(2)}, u32[]{:S(2)}) collective-permute-start(bf16[256,2304]{1,0:T(8,128)(2,1)} %get-tuple-element.64.d_own_ref.refs_0_), channel_id=1, source_target_pairs={{0,1},{1,2},{2,3},{4,5},{5,6},{6,7},{8,9},{9,10},{10,11},{12,13},{... | collective-permute-start | bytes 3538952 | tf_op jit(solution)/shard_map/ppermute | solution.py:560
  81.2 34.8 %collective-permute-start.13 = (bf16[256,3072]{1,0:T(8,128)(2,1)S(1)}, bf16[256,3072]{1,0:T(8,128)(2,1)S(1)}, u32[]{:S(2)}, u32[]{:S(2)}) collective-permute-start(bf16[256,3072]{1,0:T(8,128)(2,1)S(1)} %pad_maximum_fusion.1), channel_id=1, source_target_pairs={{0,8},{4,12},{8,0},{12,4},{1,9},{5,13},{9,1},{13,5},{2,10},{6,14},... | collective-permute-start | bytes 4718600 | tf_op jit(solution)/shard_map/ppermute | solution.py:20
  82.9 22.8 %collective-permute-start.14 = (bf16[1024,384]{1,0:T(8,128)(2,1)S(1)}, bf16[1024,384]{1,0:T(8,128)(2,1)S(1)}, u32[]{:S(2)}, u32[]{:S(2)}) collective-permute-start(bf16[1024,384]{1,0:T(8,128)(2,1)S(1)} %constant_dynamic-update-slice_fusion.x_own_ref), channel_id=1, source_target_pairs={{0,4},{4,0},{8,12},{12,8},{1,5},{5,1},{9,13},{13,9},{2,6},{6,2},{1... | collective-permute-start | bytes 2359304 | tf_op jit(solution)/shard_map/ppermute | solution.py:20
  116.0 29.4 %collective-permute-start.15 = (bf16[256,2304]{1,0:T(8,128)(2,1)}, bf16[256,2304]{1,0:T(8,128)(2,1)S(1)}, u32[]{:S(2)}, u32[]{:S(2)}) collective-permute-start(bf16[256,2304]{1,0:T(8,128)(2,1)} %collective-permute-done.11), channel_id=1, source_target_pairs={{1,0},{2,1},{5,4},{6,5},{9,8},{10,9},{13,12},{14,13},{17,16},{18,1... | collective-permute-start | bytes 3538952 | tf_op jit(solution)/shard_map/ppermute | solution.py:559
  117.2 28.1 %collective-permute-start.16 = (bf16[256,2304]{1,0:T(8,128)(2,1)}, bf16[256,2304]{1,0:T(8,128)(2,1)}, u32[]{:S(2)}, u32[]{:S(2)}) collective-permute-start(bf16[256,2304]{1,0:T(8,128)(2,1)} %collective-permute-done.12), channel_id=1, source_target_pairs={{1,2},{2,3},{5,6},{6,7},{9,10},{10,11},{13,14},{14,15},{17,18},{18... | collective-permute-start | bytes 3538952 | tf_op jit(solution)/shard_map/ppermute | solution.py:560
  119.0 27.6 %collective-permute-start.17 = (bf16[256,2304]{1,0:T(8,128)(2,1)}, bf16[256,2304]{1,0:T(8,128)(2,1)}, u32[]{:S(2)}, u32[]{:S(2)}) collective-permute-start(bf16[256,2304]{1,0:T(8,128)(2,1)} %select_select_fusion.refs_1_), channel_id=1, source_target_pairs={{0,8},{4,12},{8,0},{12,4},{1,9},{5,13},{9,1},{13,5},{2,10},{6,14},... | collective-permute-start | bytes 3538952 | tf_op jit(solution)/shard_map/ppermute | solution.py:20
  147.5 32.7 %collective-permute-start.20 = (bf16[256,2304]{1,0:T(8,128)(2,1)S(1)}, bf16[256,2304]{1,0:T(8,128)(2,1)S(1)}, u32[]{:S(2)}, u32[]{:S(2)}) collective-permute-start(bf16[256,2304]{1,0:T(8,128)(2,1)S(1)} %collective-permute-done.15), channel_id=1, source_target_pairs={{1,0},{5,4},{9,8},{13,12},{17,16},{21,20},{25,24},{29,28}} | collective-permute-start | bytes 3538952 | tf_op jit(solution)/shard_map/ppermute | solution.py:559
  148.8 33.3 %collective-permute-start.23 = (bf16[256,1536]{1,0:T(8,128)(2,1)S(1)}, bf16[256,1536]{1,0:T(8,128)(2,1)S(1)}, u32[]{:S(2)}, u32[]{:S(2)}) collective-permute-start(bf16[256,1536]{1,0:T(8,128)(2,1)S(1)} %copy-done.18), channel_id=1, source_target_pairs={{0,4},{4,0},{8,12},{12,8},{1,5},{5,1},{9,13},{13,9},{2,6},{6,2},{1... | collective-permute-start | bytes 2359304 | tf_op jit(solution)/shard_map/ppermute | solution.py:20
  149.3 47.7 %collective-permute-start.18 = (bf16[256,2304]{1,0:T(8,128)(2,1)}, bf16[256,2304]{1,0:T(8,128)(2,1)}, u32[]{:S(2)}, u32[]{:S(2)}) collective-permute-start(bf16[256,2304]{1,0:T(8,128)(2,1)} %select_select_fusion.2.refs_2_), channel_id=1, source_target_pairs={{0,8},{4,12},{8,0},{12,4},{1,9},{5,13},{9,1},{13,5},{2,10},{6,14},... | collective-permute-start | bytes 3538952 | tf_op jit(solution)/shard_map/ppermute | solution.py:20
  181.6 28.0 %collective-permute-start.22 = (bf16[256,2304]{1,0:T(8,128)(2,1)}, bf16[256,2304]{1,0:T(8,128)(2,1)S(1)}, u32[]{:S(2)}, u32[]{:S(2)}) collective-permute-start(bf16[256,2304]{1,0:T(8,128)(2,1)} %select_select_fusion.1.refs_3_), channel_id=1, source_target_pairs={{0,8},{4,12},{8,0},{12,4},{1,9},{5,13},{9,1},{13,5},{2,10},{6,14},... | collective-permute-start | bytes 3538952 | tf_op jit(solution)/shard_map/ppermute | solution.py:20
  184.7 34.8 %collective-permute-start.24 = (bf16[256,1536]{1,0:T(8,128)(2,1)S(1)}, bf16[256,1536]{1,0:T(8,128)(2,1)S(1)}, u32[]{:S(2)}, u32[]{:S(2)}) collective-permute-start(bf16[256,1536]{1,0:T(8,128)(2,1)S(1)} %copy-done.17), channel_id=1, source_target_pairs={{1,0},{5,4},{9,8},{13,12},{17,16},{21,20},{25,24},{29,28}} | collective-permute-start | bytes 2359304 | tf_op jit(solution)/shard_map/ppermute | solution.py:559
  186.0 33.5 %collective-permute-start.25 = (bf16[256,1536]{1,0:T(8,128)(2,1)}, bf16[256,1536]{1,0:T(8,128)(2,1)S(1)}, u32[]{:S(2)}, u32[]{:S(2)}) collective-permute-start(bf16[256,1536]{1,0:T(8,128)(2,1)} %collective-permute-done.7), channel_id=1, source_target_pairs={{2,3},{6,7},{10,11},{14,15},{18,19},{22,23},{26,27},{30,31}} | collective-permute-start | bytes 2359304 | tf_op jit(solution)/shard_map/ppermute | solution.py:560
  186.8 32.7 %collective-permute-start.26 = (bf16[256,384]{1,0:T(8,128)(2,1)S(1)}, bf16[256,384]{1,0:T(8,128)(2,1)S(1)}, u32[]{:S(2)}, u32[]{:S(2)}) collective-permute-start(bf16[256,384]{1,0:T(8,128)(2,1)S(1)} %get-tuple-element.126), channel_id=1, source_target_pairs={{0,3},{1,0},{2,1},{3,2},{4,7},{5,4},{6,5},{7,6},{8,11},{9,8},{10,9... | collective-permute-start | bytes 589832 | tf_op jit(solution)/shard_map/ppermute | solution.py:606
  196.9 22.5 %collective-permute-start.27 = (bf16[256,384]{1,0:T(8,128)(2,1)S(1)}, bf16[256,384]{1,0:T(8,128)(2,1)S(1)}, u32[]{:S(2)}, u32[]{:S(2)}) collective-permute-start(bf16[256,384]{1,0:T(8,128)(2,1)S(1)} %get-tuple-element.125), channel_id=1, source_target_pairs={{0,2},{1,3},{2,0},{3,1},{4,6},{5,7},{6,4},{7,5},{8,10},{9,11},{10,... | collective-permute-start | bytes 589832 | tf_op jit(solution)/shard_map/ppermute | solution.py:606
  (27 other events, 201.0 us)
